TPU v7x, 32 devices: a whole 2x2x4 slice. The times are simulated.
32 devices in a mesh: dp: 4 (over z), graph: 8 (over y, x, core).
Axes of the slice: x: 2, y: 2, z: 4, core: 2. Of those that a mesh axis runs over, the one named last changes fastest.
Arguments:
- features: float32 [4, 128, 3200], P('dp', 'graph'), may hold values from -6 to 6
- cotangent: float32 [4, 128, 1600], P('dp', 'graph'), may hold values from -6 to 6
- rotation: bfloat16 [4, 114, 1536], P('dp', None, 'graph'), may hold values from -2.6875 to 2.6875
- send_left: int32 [4, 64], P('dp', 'graph'), may hold values from 0 to 16, as said below
- send_right: int32 [4, 64], P('dp', 'graph'), may hold values from 0 to 16, as said below
- edge_src: int32 [4, 1536], P('dp', 'graph'), may hold values from 0 to 31, as said below
- edge_tgt: int32 [4, 1536], P('dp', 'graph'), may hold values from 0 to 15, as said below
- w_zero: bfloat16 [640, 832], P('graph'), may hold values from -0.25 to 0.25
- w_one_re: bfloat16 [512, 256], P('graph'), may hold values from -0.1875 to 0.1875
- w_one_im: bfloat16 [512, 256], P('graph'), may hold values from -0.1875 to 0.1875
- w_two_re: bfloat16 [384, 192], P('graph'), may hold values from -0.21875 to 0.21875
- w_two_im: bfloat16 [384, 192], P('graph'), may hold values from -0.21875 to 0.21875
- w_target: bfloat16 [128, 512], P('graph'), may hold values from -0.5 to 0.5
- alpha_vec: bfloat16 [64, 8], P('graph'), may hold values from -0.75 to 0.75
Outputs:
- attended: bfloat16 [4, 128, 1600], P('dp', 'graph')
- grad_features: float32 [4, 128, 3200], P('dp', 'graph')
- grad_zero: float32 [640, 832], P('graph')
- grad_one_re: float32 [512, 256], P('graph')
- grad_one_im: float32 [512, 256], P('graph')
- grad_two_re: float32 [384, 192], P('graph')
- grad_two_im: float32 [384, 192], P('graph')
- grad_target: float32 [128, 512], P('graph')
- grad_alpha: float32 [64, 8], P('graph')
Inputs may be any that keep to these rules, and one draw needn't show every extreme that they name: `send_left`: filled slots come first and name distinct atoms; the value 16 marks an empty slot; each list holds 4 or more atoms, and in every cell some slab fills all 8 slots. `send_right`: like send_left. `edge_src`: values below 16 are the slab's own atoms; 16 + k is slot k of slab g-1's send_right, 24 + k slot k of slab g+1's send_left; never an empty slot. `edge_tgt`: every atom of a slab is the target of one edge or more.
All inputs are finite; a program needn't handle non-finite values.
Results may differ from a plain program's by a relative error of at most 0.0085.
Values may be sent and summed in bfloat16 or wider, within the bound.
A program may use at most 128 MiB of HBM per device.

v0:
```python
from functools import partial

import jax
import jax.numpy as jnp
from jax import lax
from jax.experimental import pallas as pl
from jax.experimental.pallas import tpu as pltpu
from jax.sharding import PartitionSpec as P

F32 = jnp.float32
BF16 = jnp.bfloat16
OFFSETS = {1: 0, 2: 9, 3: 34, 4: 69}
DEGREES = (1, 2, 3, 4)
BLOCK_C = 32
BLOCK_H = 16


def slot(degree, azimuth):
    return {0: degree, 1: 4 + degree, -1: 8 + degree, 2: 11 + degree, -2: 14 + degree}[azimuth]


def orders(degree):
    kept = min(degree, 2)
    return range(-kept, kept + 1)


def rot_row(degree, azimuth, column):
    return OFFSETS[degree] + (azimuth + min(degree, 2)) * (2 * degree + 1) + column


def dot(a, b, ca, cb, precision=None):
    return lax.dot_general(
        a, b, (((ca,), (cb,)), ((), ())), preferred_element_type=F32, precision=precision
    )


def compute_kernel(
    feat_ref, near_ref, cot_ref, rotation_ref, src_ref, tgt_ref,
    wz_ref, w1r_ref, w1i_ref, w2r_ref, w2i_ref, wt_ref, alpha_ref,
    att_ref, own_ref, ghost_ref, gz_ref, g1r_ref, g1i_ref, g2r_ref, g2i_ref, gt_ref, ga_ref,
    ext_ref, alphas, d_alphas, rotf, xs, turned, hid, msg, dmsg, scores, dhid, dmixed, dturned, dxs, small, spreads,
):
    edges = rotation_ref.shape[1]
    rows = ext_ref.shape[0]
    atoms = att_ref.shape[0]
    channels = wt_ref.shape[0]
    hidden = w1r_ref.shape[1] // 4
    heads = small.shape[1]
    width = alphas.shape[0]
    pieces, piece_rows = alpha_ref.shape[:2]

    ext_ref[:atoms, :] = feat_ref[...].astype(BF16)
    ext_ref[atoms:, :] = near_ref[...].astype(F32).reshape(rows - atoms, -1).astype(BF16)
    for j in range(pieces):
        alphas[j * piece_rows:(j + 1) * piece_rows, :] = alpha_ref[j].astype(F32)

    rotf[...] = rotation_ref[...].astype(F32)
    src_hot = (
        lax.broadcasted_iota(jnp.int32, (rows, edges), 0) == src_ref[...]
    ).astype(F32).astype(BF16)
    member = (lax.broadcasted_iota(jnp.int32, (atoms, edges), 0) == tgt_ref[...]).astype(F32)
    member_b = member.astype(BF16)

    for k in range(25):
        xs[k] = dot(ext_ref[:, k * channels:(k + 1) * channels], src_hot, 0, 0)
        dmsg[k] = dot(
            cot_ref[:, k * hidden:(k + 1) * hidden].astype(BF16), member_b, 0, 0
        )

    def turn(i, carry):
        part = pl.ds(pl.multiple_of(i * BLOCK_C, BLOCK_C), BLOCK_C)
        turned[0, part, :] = xs[0, part, :].astype(BF16)
        for degree in DEGREES:
            for azimuth in orders(degree):
                total = None
                for n in range(2 * degree + 1):
                    k = rot_row(degree, azimuth, n)
                    term = rotf[k:k + 1, :] * xs[degree * degree + n, part, :]
                    total = term if total is None else total + term
                turned[slot(degree, azimuth), part, :] = total.astype(BF16)
        return carry

    lax.fori_loop(0, channels // BLOCK_C, turn, 0)

    zero_in = turned[0:5].reshape(5 * channels, edges)
    one_pos = turned[5:9].reshape(4 * channels, edges)
    one_neg = turned[9:13].reshape(4 * channels, edges)
    two_pos = turned[13:16].reshape(3 * channels, edges)
    two_neg = turned[16:19].reshape(3 * channels, edges)

    hid[0:5] = dot(wz_ref[:, :5 * hidden], zero_in, 0, 0).reshape(5, hidden, edges)
    per_atom = dot(ext_ref[:atoms, :channels], wt_ref[...], 1, 0)
    high = per_atom.astype(BF16)
    low = (per_atom - high.astype(F32)).astype(BF16)
    scores[...] = (
        dot(wz_ref[:, 5 * hidden:], zero_in, 0, 0)
        + dot(high, member_b, 0, 0)
        + dot(low, member_b, 0, 0)
    )
    hid[5:9] = (dot(w1r_ref[...], one_pos, 0, 0) - dot(w1i_ref[...], one_neg, 0, 0)).reshape(
        4, hidden, edges)
    hid[9:13] = (dot(w1r_ref[...], one_neg, 0, 0) + dot(w1i_ref[...], one_pos, 0, 0)).reshape(
        4, hidden, edges)
    hid[13:16] = (dot(w2r_ref[...], two_pos, 0, 0) - dot(w2i_ref[...], two_neg, 0, 0)).reshape(
        3, hidden, edges)
    hid[16:19] = (dot(w2r_ref[...], two_neg, 0, 0) + dot(w2i_ref[...], two_pos, 0, 0)).reshape(
        3, hidden, edges)

    for h in range(heads):
        part = slice(h * width, (h + 1) * width)
        value = scores[part, :]
        centre = value - jnp.mean(value, axis=0, keepdims=True)
        scale = lax.rsqrt(jnp.mean(centre * centre, axis=0, keepdims=True) + 1e-05)
        normed = centre * scale
        scores[part, :] = normed
        gate = 0.2 + 0.8 * jax.nn.sigmoid(normed)
        small[0, h:h + 1, :] = jnp.sum(
            normed * gate * alphas[:, h:h + 1], axis=0, keepdims=True
        )
        small[1, h:h + 1, :] = scale

    exact = lax.Precision.HIGHEST
    raised = jnp.exp(small[0])
    totals = dot(dot(raised, member, 1, 1, exact), member, 1, 0, exact)
    weights = raised / totals
    spreads[0] = jnp.broadcast_to(
        weights[:, None, :], (heads, hidden // heads, edges)
    ).reshape(hidden, edges)

    def mix(i, carry):
        part = pl.ds(pl.multiple_of(i * BLOCK_H, BLOCK_H), BLOCK_H)
        spread = spreads[0, part, :]
        scalar = hid[0, part, :]
        gating = jax.nn.sigmoid(scalar)
        silu = scalar * gating
        both = gating * spread
        msg[0, part, :] = (silu * spread).astype(BF16)
        d_first = dmsg[0, part, :]
        inner = jnp.zeros_like(scalar)
        for degree in DEGREES:
            size = 2 * degree + 1
            sums = [None] * size
            for azimuth in orders(degree):
                raw = hid[slot(degree, azimuth), part, :]
                value = raw * both
                back = None
                for n in range(size):
                    k = rot_row(degree, azimuth, n)
                    line = rotf[k:k + 1, :]
                    term = line * value
                    sums[n] = term if sums[n] is None else sums[n] + term
                    other = line * dmsg[degree * degree + n, part, :]
                    back = other if back is None else back + other
                inner = inner + back * raw
                dhid[slot(degree, azimuth), part, :] = (back * both).astype(BF16)
            for n in range(size):
                msg[degree * degree + n, part, :] = sums[n].astype(BF16)
        spreads[1, part, :] = inner * gating + d_first * silu
        d_scalar = d_first * spread * gating * (1.0 + scalar * (1.0 - gating)) + (
            inner * spread * gating * (1.0 - gating)
        )
        dhid[0, part, :] = d_scalar.astype(BF16)
        return carry

    lax.fori_loop(0, hidden // BLOCK_H, mix, 0)

    att_ref[...] = dot(member_b, msg[...].reshape(25 * hidden, edges), 1, 1).astype(BF16)

    d_weights = jnp.sum(
        spreads[1].reshape(heads, hidden // heads, edges), axis=1
    )
    product = weights * d_weights
    d_logits = product - weights * dot(
        dot(product, member, 1, 1, exact), member, 1, 0, exact
    )
    small[0] = d_logits
    for h in range(heads):
        part = slice(h * width, (h + 1) * width)
        normed = scores[part, :]
        sig = jax.nn.sigmoid(normed)
        gate = 0.2 + 0.8 * sig
        d_logit = small[0, h:h + 1, :]
        d_alphas[:, h:h + 1] = jnp.sum(normed * gate * d_logit, axis=1, keepdims=True)
        d_norm = d_logit * alphas[:, h:h + 1] * (gate + 0.8 * normed * sig * (1.0 - sig))
        first = jnp.mean(d_norm, axis=0, keepdims=True)
        second = jnp.mean(d_norm * normed, axis=0, keepdims=True)
        d_score = small[1, h:h + 1, :] * (d_norm - first - normed * second)
        dmixed[5 * hidden + h * width:5 * hidden + (h + 1) * width, :] = d_score.astype(BF16)
        scores[part, :] = d_score
    for j in range(pieces):
        ga_ref[j] = d_alphas[j * piece_rows:(j + 1) * piece_rows, :].astype(BF16)
    dmixed[:5 * hidden, :] = dhid[0:5].reshape(5 * hidden, edges)

    d_per_atom = dot(member, scores[...], 1, 1, exact).astype(BF16)
    gt_ref[...] = dot(ext_ref[:atoms, :channels], d_per_atom, 0, 0).astype(BF16)
    d_target = dot(d_per_atom, wt_ref[...], 1, 1)

    gz_ref[...] = dot(zero_in, dmixed[...], 1, 1).astype(BF16)
    dturned[0:5] = dot(wz_ref[...], dmixed[...], 1, 0).reshape(5, channels, edges)

    def pair(first, count, re_ref, im_ref, gre_ref, gim_ref, pos, neg):
        middle = first + count
        last = middle + count
        up = dhid[first:middle].reshape(count * hidden, edges)
        down = dhid[middle:last].reshape(count * hidden, edges)
        gre_ref[...] = (dot(pos, up, 1, 1) + dot(neg, down, 1, 1)).astype(BF16)
        gim_ref[...] = (dot(pos, down, 1, 1) - dot(neg, up, 1, 1)).astype(BF16)
        dturned[first:middle] = (
            dot(re_ref[...], up, 1, 0) + dot(im_ref[...], down, 1, 0)
        ).reshape(count, channels, edges)
        dturned[middle:last] = (
            dot(re_ref[...], down, 1, 0) - dot(im_ref[...], up, 1, 0)
        ).reshape(count, channels, edges)

    pair(5, 4, w1r_ref, w1i_ref, g1r_ref, g1i_ref, one_pos, one_neg)
    pair(13, 3, w2r_ref, w2i_ref, g2r_ref, g2i_ref, two_pos, two_neg)

    def turn_back(i, carry):
        part = pl.ds(pl.multiple_of(i * BLOCK_C, BLOCK_C), BLOCK_C)
        dxs[0, part, :] = dturned[0, part, :].astype(BF16)
        for degree in DEGREES:
            for n in range(2 * degree + 1):
                total = None
                for azimuth in orders(degree):
                    k = rot_row(degree, azimuth, n)
                    term = rotf[k:k + 1, :] * dturned[slot(degree, azimuth), part, :]
                    total = term if total is None else total + term
                dxs[degree * degree + n, part, :] = total.astype(BF16)
        return carry

    lax.fori_loop(0, channels // BLOCK_C, turn_back, 0)

    ext_grad = dot(src_hot, dxs[...].reshape(25 * channels, edges), 1, 1)
    own_ref[...] = ext_grad[:atoms]
    own_ref[:, :channels] = ext_grad[:atoms, :channels] + d_target
    slots = ghost_ref.shape[1]
    for side in range(2):
        begin = atoms + side * slots
        ghost_ref[side] = ext_grad[begin:begin + slots].astype(BF16)


def compute(features, near, cot, rotation, src, tgt, wz, w1r, w1i, w2r, w2i, wt, alpha):
    edges = rotation.shape[1]
    atoms = cot.shape[0]
    pieces, piece_rows, heads = alpha.shape
    head_width = pieces * piece_rows
    channels = wt.shape[0]
    hidden = w1r.shape[1] // 4
    shape = jax.ShapeDtypeStruct
    vmem = pl.BlockSpec(memory_space=pltpu.VMEM)
    out_shape = (
        shape((atoms, 25 * hidden), BF16),
        shape((atoms, 25 * channels), F32),
        shape(near.shape, BF16),
        shape(wz.shape, BF16),
        shape(w1r.shape, BF16),
        shape(w1i.shape, BF16),
        shape(w2r.shape, BF16),
        shape(w2i.shape, BF16),
        shape(wt.shape, BF16),
        shape(alpha.shape, BF16),
    )
    scratch = [
        pltpu.VMEM((atoms + 2 * near.shape[1], 25 * channels), BF16),
        pltpu.VMEM((head_width, heads), F32),
        pltpu.VMEM((head_width, heads), F32),
        pltpu.VMEM(rotation.shape, F32),
        pltpu.VMEM((25, channels, edges), F32),
        pltpu.VMEM((19, channels, edges), BF16),
        pltpu.VMEM((19, hidden, edges), F32),
        pltpu.VMEM((25, hidden, edges), BF16),
        pltpu.VMEM((25, hidden, edges), F32),
        pltpu.VMEM((head_width * heads, edges), F32),
        pltpu.VMEM((19, hidden, edges), BF16),
        pltpu.VMEM((wz.shape[1], edges), BF16),
        pltpu.VMEM((19, channels, edges), F32),
        pltpu.VMEM((25, channels, edges), BF16),
        pltpu.VMEM((2, heads, edges), F32),
        pltpu.VMEM((2, hidden, edges), F32),
    ]
    return pl.pallas_call(
        compute_kernel,
        out_shape=out_shape,
        in_specs=[vmem] * 13,
        out_specs=[vmem] * 10,
        scratch_shapes=scratch,
        compiler_params=pltpu.CompilerParams(vmem_limit_bytes=56 * 2**20),
        name="slab",
    )(features, near, cot, rotation, src, tgt, wz, w1r, w1i, w2r, w2i, wt, alpha)


MESH = pl.DeviceIdType.MESH


def greet(n, depth):
    me = lax.axis_index("graph")
    row = lax.axis_index("dp")
    barrier = pltpu.get_barrier_semaphore()
    for d in range(1, n):
        pl.semaphore_signal(
            barrier, inc=1, device_id=(row, lax.rem(me + d, n)), device_id_type=MESH)
    for d in range(1, depth):
        pl.semaphore_signal(
            barrier, inc=1, device_id=(lax.rem(row + d, depth), me), device_id_type=MESH)
    pl.semaphore_wait(barrier, n - 1 + depth - 1)


def gather_kernel(n, count, *refs):
    shards = refs[:count]
    feat_ref, left_ref, right_ref = refs[count:count + 3]
    full = refs[count + 3:2 * count + 3]
    ghosts = refs[2 * count + 3]
    outgoing, send_sem, recv_sem, pass_sem, local_sem, side_send, side_recv = refs[2 * count + 4:]
    me = lax.axis_index("graph")
    row = lax.axis_index("dp")
    half = n // 2
    sibling = me + 1 - 2 * lax.rem(me, 2)
    right, left = lax.rem(me + 1, n), lax.rem(me + n - 1, n)
    own = feat_ref[...].astype(BF16)
    for side, list_ref in ((0, left_ref), (1, right_ref)):
        ids = lax.broadcasted_iota(jnp.int32, (own.shape[0], list_ref.shape[1]), 0)
        pick = (ids == list_ref[...]).astype(F32).astype(BF16)
        outgoing[side] = dot(pick, own, 0, 0).astype(BF16)
    greet(n, 1)

    def remote(src, dst, send, recv, target):
        copy = pltpu.make_async_remote_copy(
            src_ref=src, dst_ref=dst, send_sem=send, recv_sem=recv,
            device_id=(row, target), device_id_type=MESH)
        copy.start()
        return copy

    sends = []
    direct = []
    for d in range(1, half):
        target = lax.rem(me + 2 * d, n)
        for w in range(count):
            direct.append(remote(shards[w], full[w].at[me], send_sem.at[d, w],
                                 recv_sem.at[d, w], target))
    locals_ = []
    for w in range(count):
        copy = pltpu.make_async_copy(shards[w], full[w].at[me], local_sem.at[w])
        copy.start()
        locals_.append(copy)
        sends.append(remote(shards[w], full[w].at[me], send_sem.at[0, w],
                            recv_sem.at[0, w], sibling))
    for side, target in ((1, left), (0, right)):
        sends.append(remote(outgoing.at[1 - side], ghosts.at[side], side_send.at[side],
                            side_recv.at[side], target))
    for d in range(1, half):
        source = lax.rem(me + n - 2 * d, n)
        for w in range(count):
            direct[(d - 1) * count + w].wait_recv()
            sends.append(remote(full[w].at[source], full[w].at[source], pass_sem.at[0, d, w],
                                pass_sem.at[1, d, w], sibling))
    for copy in direct:
        copy.wait_send()
    for copy in locals_:
        copy.wait()
    for copy in sends:
        copy.wait()


def gather(n, shards, features, send_left, send_right):
    count = len(shards)
    vmem = pl.BlockSpec(memory_space=pltpu.VMEM)
    shapes = [jax.ShapeDtypeStruct((n, *s.shape), s.dtype) for s in shards]
    ghosts = (2, send_left.shape[1], features.shape[1])
    shapes.append(jax.ShapeDtypeStruct(ghosts, BF16))
    dma = pltpu.SemaphoreType.DMA
    return pl.pallas_call(
        partial(gather_kernel, n, count),
        out_shape=tuple(shapes),
        in_specs=[vmem] * (count + 3),
        out_specs=[vmem] * (count + 1),
        scratch_shapes=[pltpu.VMEM(ghosts, BF16),
                        dma((n // 2, count)), dma((n // 2, count)), dma((2, n // 2, count)),
                        dma((count,)), dma((2,)), dma((2,))],
        compiler_params=pltpu.CompilerParams(collective_id=0, has_side_effects=True),
        name="fetch",
    )(*shards, features, send_left, send_right)


def reduce_kernel(n, depth, count, *refs):
    terms = refs[:count]
    ghosts = refs[count]
    final = refs[count + 1:2 * count + 1]
    back = refs[2 * count + 1]
    rest = refs[2 * count + 2:]
    landed = rest[:count]
    partial_sums = rest[count:2 * count]
    arrived = rest[2 * count:3 * count]
    layers = rest[3 * count:4 * count]
    incoming = rest[4 * count:5 * count]
    (core_send, core_recv, chip_send, chip_recv, deep_send, deep_recv, last_send, last_recv,
     side_send, side_recv) = rest[5 * count:]
    me = lax.axis_index("graph")
    row = lax.axis_index("dp")
    half = n // 2
    parity = lax.rem(me, 2)
    chip = lax.div(me, 2)
    sibling = me + 1 - 2 * parity
    right, left = lax.rem(me + 1, n), lax.rem(me + n - 1, n)
    greet(n, depth)

    def remote(src, dst, send, recv, target):
        copy = pltpu.make_async_remote_copy(
            src_ref=src, dst_ref=dst, send_sem=send, recv_sem=recv,
            device_id=target, device_id_type=MESH)
        copy.start()
        return copy

    order = list(range(1, half)) + [0]
    first, second, third, fourth = {}, {}, {}, {}
    for w in range(count):
        for d in order:
            spot = lax.rem(chip + d, half)
            first[d, w] = remote(
                terms[w].at[2 * spot + 1 - parity], landed[w].at[d],
                core_send.at[d, w], core_recv.at[d, w], (row, sibling))
    for w in range(count):
        for d in order:
            target = lax.rem(me + 2 * d, n)
            first[d, w].wait_recv()
            partial_sums[w][d] = (
                terms[w][target].astype(F32) + landed[w][d].astype(F32)
            ).astype(BF16)
            if d:
                second[d, w] = remote(
                    partial_sums[w].at[d], arrived[w].at[d],
                    chip_send.at[d, w], chip_recv.at[d, w], (row, target))
    sides = [
        remote(ghosts.at[0], back.at[0], side_send.at[0], side_recv.at[0], (row, left)),
        remote(ghosts.at[1], back.at[1], side_send.at[1], side_recv.at[1], (row, right)),
    ]
    split = [final[w].shape[1] != terms[w].shape[1]
             for w in range(count)]
    for w in range(count):
        total = partial_sums[w][0].astype(F32)
        for d in range(1, half):
            second[d, w].wait_recv()
            total = total + arrived[w][d].astype(F32)
        if split[w]:
            size = total.shape[0] // depth
            for k in range(depth):
                layers[w][k] = total[k * size:(k + 1) * size].astype(BF16)
            for z in range(1, depth):
                target = lax.rem(row + z, depth)
                third[z, w] = remote(
                    layers[w].at[target], incoming[w].at[z],
                    deep_send.at[z, w], deep_recv.at[z, w], (target, me))
        else:
            final[w][row] = total.astype(BF16)
    for w in range(count):
        if split[w]:
            total = layers[w][row].astype(F32)
            for z in range(1, depth):
                third[z, w].wait_recv()
                total = total + incoming[w][z].astype(F32)
            final[w][row] = total.astype(BF16)
        for z in range(1, depth):
            fourth[z, w] = remote(
                final[w].at[row], final[w].at[row],
                last_send.at[z, w], last_recv.at[z, w], (lax.rem(row + z, depth), me))
    for group in (first, second, third):
        for copy in group.values():
            copy.wait_send()
    for copy in sides:
        copy.wait()
    for copy in fourth.values():
        copy.wait()


def reduce(n, depth, terms, ghosts):
    count = len(terms)
    half = n // 2
    vmem = pl.BlockSpec(memory_space=pltpu.VMEM)

    def layered(t):
        rows = t.shape[1] if t.shape[1] % depth else t.shape[1] // depth
        return (depth, rows, t.shape[2])

    shapes = [jax.ShapeDtypeStruct(layered(t), BF16) for t in terms]
    shapes.append(jax.ShapeDtypeStruct(ghosts.shape, ghosts.dtype))
    dma = pltpu.SemaphoreType.DMA
    scratch = [pltpu.VMEM((half, *t.shape[1:]), BF16) for _ in range(3) for t in terms]
    scratch += [pltpu.VMEM(layered(t), BF16) for _ in range(2) for t in terms]
    scratch += [dma((half, count)) for _ in range(4)]
    scratch += [dma((depth, count)) for _ in range(4)]
    scratch += [dma((2,)), dma((2,))]
    return pl.pallas_call(
        partial(reduce_kernel, n, depth, count),
        out_shape=tuple(shapes),
        in_specs=[vmem] * (count + 1),
        out_specs=[vmem] * (count + 1),
        scratch_shapes=scratch,
        compiler_params=pltpu.CompilerParams(collective_id=1, has_side_effects=True),
        name="combine",
    )(*terms, ghosts)


def finish_kernel(count, *refs):
    own_ref, back_ref, left_ref, right_ref = refs[:4]
    final = refs[4:4 + count]
    out_ref = refs[4 + count]
    grads = refs[5 + count:]
    total = own_ref[...]
    for side, list_ref in ((0, right_ref), (1, left_ref)):
        ids = lax.broadcasted_iota(jnp.int32, (total.shape[0], list_ref.shape[1]), 0)
        put = (ids == list_ref[...]).astype(F32).astype(BF16)
        total = total + dot(put, back_ref[side], 1, 0)
    out_ref[...] = total
    for source, grad in zip(final, grads):
        depth, size = source.shape[:2]
        if size == grad.shape[0]:
            value = source[0].astype(F32)
            for k in range(1, depth):
                value = value + source[k].astype(F32)
            grad[...] = value
        else:
            for k in range(depth):
                grad[k * size:(k + 1) * size, :] = source[k].astype(F32)


def finish(own, back, send_left, send_right, final, weights):
    count = len(final)
    vmem = pl.BlockSpec(memory_space=pltpu.VMEM)
    shapes = [jax.ShapeDtypeStruct(own.shape, F32)]
    shapes += [jax.ShapeDtypeStruct(w.shape, F32) for w in weights]
    return pl.pallas_call(
        partial(finish_kernel, count),
        out_shape=tuple(shapes),
        in_specs=[vmem] * (count + 4),
        out_specs=[vmem] * (count + 1),
        name="finish",
    )(own, back, send_left, send_right, *final)


def body(n, depth, features, cotangent, rotation, send_left, send_right, edge_src, edge_tgt,
         *weights):
    *full, near = gather(n, weights, features[0], send_left, send_right)
    matrices = [f.reshape(-1, f.shape[2]) for f in full[:6]]
    attended, own_grad, ghost_grad, *terms = compute(
        features[0], near, cotangent[0], rotation[0], edge_src, edge_tgt, *matrices, full[6])
    terms = [t.reshape(n, -1, t.shape[-1]) for t in terms]
    *final, back = reduce(n, depth, terms, ghost_grad)
    grad_features, *grads = finish(own_grad, back, send_left, send_right, final, weights)
    return (attended[None], grad_features[None], *grads)


def solution(mesh):
    cell = P("dp", "graph", None)
    lists = P("dp", "graph")
    shard = P("graph", None)
    in_specs = (cell, cell, P("dp", None, "graph")) + (lists,) * 4 + (shard,) * 7
    out_specs = (cell, cell) + (shard,) * 7
    return jax.shard_map(
        partial(body, mesh.shape["graph"], mesh.shape["dp"]), mesh=mesh,
        in_specs=in_specs, out_specs=out_specs, check_vma=False)
```

profile of v0, /device:TPU:0, one launch (start us, length us, event | category | flops | bytes accessed | tf_op | source)
XLA Modules:
  0.0 73.0 jit_solution(104978608375092961)
XLA Ops:
  0.6 1.5 %copy.23 = bf16[1,114,192]{2,1,0:T(8,128)(2,1)} copy(bf16[1,114,192]{1,2,0:T(8,128)(2,1)} %param.16) | data formatting | bytes 87552 | tf_op args[2]
  2.2 22.8 %fetch.1 = (bf16[8,80,832]{2,1,0:T(8,128)(2,1)}, bf16[8,64,256]{2,1,0:T(8,128)(2,1)}, bf16[8,64,256]{2,1,0:T(8,128)(2,1)}, bf16[8,48,192]{2,1,0:T(8,128)(2,1)}, ...) custom-call(bf16[80,832]{1,0:T(8,128)(2,1)} %refs_0_.1, ...), custom_call_target="tpu_custom_call" | custom-call | tf_op jit(solution)/shard_map/fetch/pallas_call | solution.py:371
  24.9 12.6 %slab.1 = (bf16[16,1600]{1,0:T(8,128)(2,1)}, f32[16,3200]{1,0:T(8,128)}, bf16[2,8,3200]{2,1,0:T(8,128)(2,1)}, bf16[640,832]{1,0:T(8,128)(2,1)}, bf16[512,256]{1,...) custom-call(f32[16,3200]{1,0:T(8,128)} %bitcast.20, ...), custom_call_target="tpu_custom_call" | custom-call | tf_op jit(solution)/shard_map/slab/pallas_call | solution.py:281
  37.5 33.3 %combine.1 = (bf16[4,20,832]{2,1,0:T(8,128)(2,1)}, bf16[4,16,256]{2,1,0:T(8,128)(2,1)}, bf16[4,16,256]{2,1,0:T(8,128)(2,1)}, bf16[4,12,192]{2,1,0:T(8,128)(2,1)}...) custom-call(bf16[8,80,832]{2,1,0:T(8,128)(2,1)} %bitcast.17, ...), custom_call_target="tpu_custom_call" | custom-call | tf_op jit(solution)/shard_map/combine/pallas_call | solution.py:491
  70.9 2.1 %finish.1 = (f32[16,3200]{1,0:T(8,128)}, f32[80,832]{1,0:T(8,128)}, f32[64,256]{1,0:T(8,128)}, f32[64,256]{1,0:T(8,128)}, f32[48,192]{1,0:T(8,128)}, /*index=5*/...) custom-call(f32[16,3200]{1,0:T(8,128)} %get-tuple-element.52.refs_0_, bf16[2,8,3200]{2,1,0:T(8,128)(2,1)} %get-tuple-element.61.refs_1_, ...), custom_call_target="tpu_custom_call" | custom-call | tf_op jit(solution)/shard_map/finish/pallas_call | solution.py:530
where the time goes:
time: 73.3 us; the launch traced here: 73 us
  Pallas kernels  70.8 us (97%)
  local copies, waits for them, and re-layouts  1.54 us (2%)
    pallas_call x1, Pallas kernels, reduce(): pl.pallas_call(partial(reduce_kernel, n, depth, count), out_shape=tuple(s...  33.3 us
    pallas_call x1, Pallas kernels, gather(): pl.pallas_call(partial(gather_kernel, n, count), out_shape=tuple(shapes),...  22.8 us
    pallas_call x1, Pallas kernels, compute(): pl.pallas_call(compute_kernel, out_shape=out_shape, in_specs=[vmem] * 13,...  12.6 us
    pallas_call x1, Pallas kernels, finish(): pl.pallas_call(partial(finish_kernel, count), out_shape=tuple(shapes), in...  2.12 us
    unnamed x1, local copies, waits for them, and re-layouts  1.54 us

commit v1 on v0

v1 whole, which is shorter than its diff:
```python
from functools import partial

import jax
import jax.numpy as jnp
from jax import lax
from jax.experimental import pallas as pl
from jax.experimental.pallas import tpu as pltpu
from jax.sharding import PartitionSpec as P

F32 = jnp.float32
BF16 = jnp.bfloat16
OFFSETS = {1: 0, 2: 9, 3: 34, 4: 69}
DEGREES = (1, 2, 3, 4)
BLOCK_C = 32
BLOCK_H = 16
MESH = pl.DeviceIdType.MESH
EXACT = lax.Precision.HIGHEST


def slot(degree, azimuth):
    return {0: degree, 1: 4 + degree, -1: 8 + degree, 2: 11 + degree, -2: 14 + degree}[azimuth]


def orders(degree):
    kept = min(degree, 2)
    return range(-kept, kept + 1)


def rot_row(degree, azimuth, column):
    return OFFSETS[degree] + (azimuth + min(degree, 2)) * (2 * degree + 1) + column


def dot(a, b, ca, cb, precision=None):
    return lax.dot_general(
        a, b, (((ca,), (cb,)), ((), ())), preferred_element_type=F32, precision=precision
    )


def flip(index, power):
    bit = lax.rem(lax.div(index, power), 2)
    return index + (1 - 2 * bit) * power


def flips(index, powers, chosen):
    for j in chosen:
        index = flip(index, powers[j])
    return index


def subsets(steps):
    found = [()]
    for j in steps:
        found = found + [s + (j,) for s in found]
    return found


class Halving:
    def __init__(self, count):
        self.steps = count.bit_length() - 1
        self.rest = [subsets(range(j + 1, self.steps)) for j in range(self.steps)]
        self.base = [0]
        for found in self.rest:
            self.base.append(self.base[-1] + len(found))

    def spot(self, step, chosen):
        return self.base[step] + self.rest[step].index(chosen)


def slab_kernel(n, depth, sizes, *refs):
    take = iter(refs)
    feat_ref, cot_ref, rot_ref, src_ref, tgt_ref, left_ref, right_ref = [next(take) for _ in range(7)]
    count = len(sizes["weights"])
    items = len(sizes["terms"])
    shards = [next(take) for _ in range(count)]
    att_ref, grad_ref = next(take), next(take)
    final = [next(take) for _ in range(items)]
    (ext_ref, alphas, d_alphas, rotf, xs, turned, hid, msg, dmsg, scores, dhid, dmixed, dturned,
     dxs, small, spreads) = [next(take) for _ in range(16)]
    outgoing, near, ghost, back = [next(take) for _ in range(4)]
    full = [next(take) for _ in range(count)]
    mats = [next(take) for _ in range(count)]
    terms = [next(take) for _ in range(items)]
    landed = [next(take) for _ in range(items)]
    out_xy = [next(take) for _ in range(items)]
    in_xy = [next(take) for _ in range(items)]
    layers = [next(take) for _ in range(items)]
    out_z = [next(take) for _ in range(items)]
    in_z = [next(take) for _ in range(items)]
    (side_send, side_recv, hop_send, hop_recv, core_send, core_recv, sib_send, sib_recv,
     xy_send, xy_recv, z_send, z_recv, last_send, last_recv) = list(take)

    edges = src_ref.shape[1]
    rows = ext_ref.shape[0]
    atoms = att_ref.shape[0]
    channels = n * sizes["weights"][5][0]
    hidden = sizes["weights"][1][1] // 4
    heads = small.shape[1]
    width = alphas.shape[0]
    slots = left_ref.shape[1]

    me = lax.axis_index("graph")
    row = lax.axis_index("dp")
    half = n // 2
    chip = lax.div(me, 2)
    parity = lax.rem(me, 2)
    sibling = me + 1 - 2 * parity
    right, left = lax.rem(me + 1, n), lax.rem(me + n - 1, n)
    plan = Halving(half)
    steps = plan.steps
    powers = [2 ** j + parity * (2 ** ((j + 1) % steps) - 2 ** j) for j in range(steps)]
    deep = Halving(depth)
    deep_powers = [2 ** j for j in range(deep.steps)]

    barrier = pltpu.get_barrier_semaphore()
    partners = [(row, sibling), (row, right), (row, left)]
    partners += [(row, 2 * flip(chip, p) + parity) for p in powers]
    partners += [(lax.rem(row + z, depth), me) for z in range(1, depth)]
    for partner in partners:
        pl.semaphore_signal(barrier, inc=1, device_id=partner, device_id_type=MESH)

    def remote(src, dst, send, recv, target):
        copy = pltpu.make_async_remote_copy(
            src_ref=src, dst_ref=dst, send_sem=send, recv_sem=recv,
            device_id=target, device_id_type=MESH)
        copy.start()
        return copy

    started = []

    own = feat_ref[...].astype(BF16)
    ext_ref[:atoms, :] = own
    for side, list_ref in ((0, left_ref), (1, right_ref)):
        ids = lax.broadcasted_iota(jnp.int32, (atoms, slots), 0)
        pick = (ids == list_ref[...]).astype(F32).astype(BF16)
        outgoing[side] = dot(pick, own, 0, 0).astype(BF16)
    for w in range(count):
        full[w][chip, parity] = shards[w][...]
    src_hot = (
        lax.broadcasted_iota(jnp.int32, (rows, edges), 0) == src_ref[...]
    ).astype(F32).astype(BF16)
    member = (lax.broadcasted_iota(jnp.int32, (atoms, edges), 0) == tgt_ref[...]).astype(F32)
    member_b = member.astype(BF16)

    pl.semaphore_wait(barrier, len(partners))

    sides = []
    for side, target in ((1, left), (0, right)):
        sides.append(remote(outgoing.at[1 - side], near.at[side], side_send.at[side],
                            side_recv.at[side], (row, target)))
    arrivals = {}

    def hop(j, w):
        target = (row, 2 * flip(chip, powers[j]) + parity)
        for t, chosen in enumerate(subsets(range(j))):
            unit = flips(chip, powers, chosen)
            source = shards[w] if j == 0 else full[w].at[unit, parity]
            copy = remote(source, full[w].at[unit, parity], hop_send.at[2 ** j + t - 1, w],
                          hop_recv.at[2 ** j + t - 1, w], target)
            arrivals[j, t, w] = copy
            started.append(copy)

    crossing = {}

    def cross(spot, unit, w, source=None):
        copy = remote(full[w].at[unit, parity] if source is None else source,
                      full[w].at[unit, parity], core_send.at[spot, w], core_recv.at[spot, w],
                      (row, sibling))
        crossing[spot, w] = copy
        started.append(copy)

    def land(j, w):
        partner = flip(chip, powers[j])
        for t, chosen in enumerate(subsets(range(j))):
            arrivals[j, t, w].wait_recv()
            cross(2 ** j + t, flips(partner, powers, chosen), w)

    weight_order = (0, 5, 6, 1, 2, 3, 4)
    for w in weight_order:
        hop(0, w)
    for w in weight_order:
        cross(0, chip, w, shards[w])

    edge_eye = (
        lax.broadcasted_iota(jnp.int32, (rot_ref.shape[1], rot_ref.shape[1]), 0)
        == lax.broadcasted_iota(jnp.int32, (rot_ref.shape[1], rot_ref.shape[1]), 1)
    ).astype(F32).astype(BF16)
    rotf[...] = dot(edge_eye, rot_ref[...], 1, 1)
    for k in range(25):
        dmsg[k] = dot(
            cot_ref[:, k * hidden:(k + 1) * hidden].astype(BF16), member_b, 0, 0
        )
    for copy in sides:
        copy.wait_recv()
    ext_ref[atoms:, :] = near[...].astype(F32).reshape(rows - atoms, -1).astype(BF16)
    for k in range(25):
        xs[k] = dot(ext_ref[:, k * channels:(k + 1) * channels], src_hot, 0, 0)

    for j in range(1, steps):
        for w in weight_order:
            land(j - 1, w)
            hop(j, w)

    def turn(i, carry):
        part = pl.ds(pl.multiple_of(i * BLOCK_C, BLOCK_C), BLOCK_C)
        turned[0, part, :] = xs[0, part, :].astype(BF16)
        for degree in DEGREES:
            for azimuth in orders(degree):
                total = None
                for m in range(2 * degree + 1):
                    k = rot_row(degree, azimuth, m)
                    term = rotf[k:k + 1, :] * xs[degree * degree + m, part, :]
                    total = term if total is None else total + term
                turned[slot(degree, azimuth), part, :] = total.astype(BF16)
        return carry

    lax.fori_loop(0, channels // BLOCK_C, turn, 0)

    zero_in = turned[0:5].reshape(5 * channels, edges)
    one_pos = turned[5:9].reshape(4 * channels, edges)
    one_neg = turned[9:13].reshape(4 * channels, edges)
    two_pos = turned[13:16].reshape(3 * channels, edges)
    two_neg = turned[16:19].reshape(3 * channels, edges)

    def settle(w):
        for spot in range(half):
            crossing[spot, w].wait_recv()
        block = sizes["weights"][w][0]
        if block % 16:
            for u in range(half):
                for c in range(2):
                    at = (2 * u + c) * block
                    mats[w][at:at + block, :] = full[w][u, c].astype(mats[w].dtype)

    def weight(w, begin=0, end=None):
        block, wide = sizes["weights"][w]
        end = wide if end is None else end
        if block % 16:
            return mats[w][:, begin:end].astype(BF16)
        return full[w][:, :, :, begin:end].reshape(n * block, end - begin)

    for w in (0, 5, 6):
        land(steps - 1, w)
    for w in (1, 2):
        land(steps - 1, w)
    for w in (0, 5, 6):
        settle(w)
    alpha_rows = sizes["weights"][6][0]
    for u in range(half):
        for c in range(2):
            at = (2 * u + c) * alpha_rows
            alphas[at:at + alpha_rows, :] = full[6][u, c].astype(F32)

    per_atom = dot(ext_ref[:atoms, :channels], weight(5), 1, 0)
    high = per_atom.astype(BF16)
    low = (per_atom - high.astype(F32)).astype(BF16)
    scores[...] = (
        dot(weight(0, 5 * hidden), zero_in, 0, 0)
        + dot(high, member_b, 0, 0)
        + dot(low, member_b, 0, 0)
    )
    hid[0:5] = dot(weight(0, 0, 5 * hidden), zero_in, 0, 0).reshape(5, hidden, edges)

    for w in (3, 4):
        land(steps - 1, w)

    for h in range(heads):
        part = slice(h * width, (h + 1) * width)
        value = scores[part, :]
        centre = value - jnp.mean(value, axis=0, keepdims=True)
        scale = lax.rsqrt(jnp.mean(centre * centre, axis=0, keepdims=True) + 1e-05)
        normed = centre * scale
        scores[part, :] = normed
        gate = 0.2 + 0.8 * jax.nn.sigmoid(normed)
        small[0, h:h + 1, :] = jnp.sum(
            normed * gate * alphas[:, h:h + 1], axis=0, keepdims=True
        )
        small[1, h:h + 1, :] = scale

    raised = jnp.exp(small[0])
    totals = dot(dot(raised, member, 1, 1, EXACT), member, 1, 0, EXACT)
    weights = raised / totals
    spreads[0] = jnp.broadcast_to(
        weights[:, None, :], (heads, hidden // heads, edges)
    ).reshape(hidden, edges)

    settle(1)
    settle(2)
    hid[5:9] = (dot(weight(1), one_pos, 0, 0) - dot(weight(2), one_neg, 0, 0)).reshape(
        4, hidden, edges)
    hid[9:13] = (dot(weight(1), one_neg, 0, 0) + dot(weight(2), one_pos, 0, 0)).reshape(
        4, hidden, edges)
    settle(3)
    settle(4)
    hid[13:16] = (dot(weight(3), two_pos, 0, 0) - dot(weight(4), two_neg, 0, 0)).reshape(
        3, hidden, edges)
    hid[16:19] = (dot(weight(3), two_neg, 0, 0) + dot(weight(4), two_pos, 0, 0)).reshape(
        3, hidden, edges)

    def mix(i, carry):
        part = pl.ds(pl.multiple_of(i * BLOCK_H, BLOCK_H), BLOCK_H)
        spread = spreads[0, part, :]
        scalar = hid[0, part, :]
        gating = jax.nn.sigmoid(scalar)
        silu = scalar * gating
        both = gating * spread
        msg[0, part, :] = (silu * spread).astype(BF16)
        d_first = dmsg[0, part, :]
        inner = jnp.zeros_like(scalar)
        for degree in DEGREES:
            size = 2 * degree + 1
            sums = [None] * size
            for azimuth in orders(degree):
                raw = hid[slot(degree, azimuth), part, :]
                value = raw * both
                back_sum = None
                for m in range(size):
                    k = rot_row(degree, azimuth, m)
                    line = rotf[k:k + 1, :]
                    term = line * value
                    sums[m] = term if sums[m] is None else sums[m] + term
                    other = line * dmsg[degree * degree + m, part, :]
                    back_sum = other if back_sum is None else back_sum + other
                inner = inner + back_sum * raw
                dhid[slot(degree, azimuth), part, :] = (back_sum * both).astype(BF16)
            for m in range(size):
                msg[degree * degree + m, part, :] = sums[m].astype(BF16)
        spreads[1, part, :] = inner * gating + d_first * silu
        d_scalar = d_first * spread * gating * (1.0 + scalar * (1.0 - gating)) + (
            inner * spread * gating * (1.0 - gating)
        )
        dhid[0, part, :] = d_scalar.astype(BF16)
        return carry

    lax.fori_loop(0, hidden // BLOCK_H, mix, 0)

    def put(i, value):
        block, wide = sizes["terms"][i]
        if block % 16:
            for u in range(half):
                for c in range(2):
                    at = (2 * u + c) * block
                    terms[i][u, c] = value[at:at + block, :].astype(BF16)
        else:
            terms[i][...] = value.astype(BF16).reshape(half, 2, block, wide)

    flights = {}
    even = [terms[i].shape[2] % depth == 0 for i in range(items)]

    def launch(key, src, dst, send, recv, target):
        copy = remote(src, dst, send, recv, target)
        flights[key] = copy
        started.append(copy)

    def to_sibling(i):
        launch(("core", i), terms[i].at[:, 1 - parity], landed[i], sib_send.at[i], sib_recv.at[i],
               (row, sibling))

    def chip_sum(i, step, chosen):
        unit = flips(chip, powers, chosen)
        total = terms[i][unit, parity].astype(F32) + landed[i][unit].astype(F32)
        for s in range(step):
            total = total + in_xy[i][plan.spot(s, chosen)].astype(F32)
        return total

    def to_chip(i, step):
        if step == 0:
            flights["core", i].wait_recv()
        else:
            flights["xy", step - 1, i].wait_recv()
        begin, end = plan.base[step], plan.base[step + 1]
        for t, rest in enumerate(plan.rest[step]):
            out_xy[i][begin + t] = chip_sum(i, step, (step,) + rest).astype(BF16)
        target = (row, 2 * flip(chip, powers[step]) + parity)
        launch(("xy", step, i), out_xy[i].at[begin:end], in_xy[i].at[begin:end],
               xy_send.at[step, i], xy_recv.at[step, i], target)

    def layer_sum(i, step, chosen):
        total = layers[i][flips(row, deep_powers, chosen)]
        for s in range(step):
            total = total + in_z[i][deep.spot(s, chosen)].astype(F32)
        return total

    def share(i):
        for z in range(1, depth):
            launch(("last", z, i), final[i].at[row], final[i].at[row], last_send.at[z, i],
                   last_recv.at[z, i], (lax.rem(row + z, depth), me))

    def to_layer(i, step):
        if step == 0:
            flights["xy", steps - 1, i].wait_recv()
            total = chip_sum(i, steps, ())
            if not even[i]:
                final[i][row] = total.astype(BF16)
                share(i)
                return
            size = total.shape[0] // depth
            for z in range(depth):
                layers[i][z] = total[z * size:(z + 1) * size]
        elif even[i]:
            flights["z", step - 1, i].wait_recv()
        if not even[i]:
            return
        if step == deep.steps:
            final[i][row] = layer_sum(i, step, ()).astype(BF16)
            share(i)
            return
        begin, end = deep.base[step], deep.base[step + 1]
        for t, rest in enumerate(deep.rest[step]):
            out_z[i][begin + t] = layer_sum(i, step, (step,) + rest).astype(BF16)
        launch(("z", step, i), out_z[i].at[begin:end], in_z[i].at[begin:end],
               z_send.at[step, i], z_recv.at[step, i], (flip(row, deep_powers[step]), me))

    def advance(i, stage):
        if stage == 0:
            to_sibling(i)
        elif stage <= steps:
            to_chip(i, stage - 1)
        else:
            to_layer(i, stage - 1 - steps)

    last_stage = steps + deep.steps + 1

    def gradient_pair(first, number, re_item, im_item, pos, neg):
        middle = first + number
        last = middle + number
        up = dhid[first:middle].reshape(number * hidden, edges)
        down = dhid[middle:last].reshape(number * hidden, edges)
        put(re_item, dot(pos, up, 1, 1) + dot(neg, down, 1, 1))
        advance(re_item, 0)
        put(im_item, dot(pos, down, 1, 1) - dot(neg, up, 1, 1))
        advance(im_item, 0)

    gradient_pair(5, 4, 0, 1, one_pos, one_neg)
    gradient_pair(13, 3, 2, 3, two_pos, two_neg)
    advance(0, 1)
    advance(1, 1)
    d_values = dhid[0:5].reshape(5 * hidden, edges)
    dmixed[:5 * hidden, :] = d_values
    put(4, dot(zero_in, d_values, 1, 1))
    advance(4, 0)
    advance(2, 1)
    advance(3, 1)

    d_weights = jnp.sum(
        spreads[1].reshape(heads, hidden // heads, edges), axis=1
    )
    product = weights * d_weights
    d_logits = product - weights * dot(
        dot(product, member, 1, 1, EXACT), member, 1, 0, EXACT
    )
    small[0] = d_logits
    for h in range(heads):
        part = slice(h * width, (h + 1) * width)
        normed = scores[part, :]
        sig = jax.nn.sigmoid(normed)
        gate = 0.2 + 0.8 * sig
        d_logit = small[0, h:h + 1, :]
        d_alphas[:, h:h + 1] = jnp.sum(normed * gate * d_logit, axis=1, keepdims=True)
        d_norm = d_logit * alphas[:, h:h + 1] * (gate + 0.8 * normed * sig * (1.0 - sig))
        first = jnp.mean(d_norm, axis=0, keepdims=True)
        second = jnp.mean(d_norm * normed, axis=0, keepdims=True)
        d_score = small[1, h:h + 1, :] * (d_norm - first - normed * second)
        dmixed[5 * hidden + h * width:5 * hidden + (h + 1) * width, :] = d_score.astype(BF16)
        scores[part, :] = d_score
    put(5, dot(zero_in, dmixed[5 * hidden:, :], 1, 1))
    advance(5, 0)
    advance(4, 1)
    d_per_atom = dot(member, scores[...], 1, 1, EXACT).astype(BF16)
    put(6, dot(ext_ref[:atoms, :channels], d_per_atom, 0, 0))
    advance(6, 0)
    for u in range(half):
        for c in range(2):
            at = (2 * u + c) * alpha_rows
            terms[7][u, c] = d_alphas[at:at + alpha_rows, :].astype(BF16)
    advance(7, 0)
    advance(0, 2)
    advance(1, 2)
    advance(5, 1)
    advance(6, 1)
    advance(7, 1)
    advance(2, 2)
    advance(3, 2)

    dturned[0:5] = dot(weight(0), dmixed[...], 1, 0).reshape(5, channels, edges)

    def turn_pair(first, number, re_item, im_item):
        middle = first + number
        last = middle + number
        up = dhid[first:middle].reshape(number * hidden, edges)
        down = dhid[middle:last].reshape(number * hidden, edges)
        dturned[first:middle] = (
            dot(weight(re_item), up, 1, 0) + dot(weight(im_item), down, 1, 0)
        ).reshape(number, channels, edges)
        dturned[middle:last] = (
            dot(weight(re_item), down, 1, 0) - dot(weight(im_item), up, 1, 0)
        ).reshape(number, channels, edges)

    turn_pair(5, 4, 1, 2)
    advance(0, 3)
    advance(1, 3)
    advance(4, 2)
    advance(5, 2)
    advance(6, 2)
    advance(7, 2)
    turn_pair(13, 3, 3, 4)

    def turn_back(i, carry):
        part = pl.ds(pl.multiple_of(i * BLOCK_C, BLOCK_C), BLOCK_C)
        dxs[0, part, :] = dturned[0, part, :].astype(BF16)
        for degree in DEGREES:
            for m in range(2 * degree + 1):
                total = None
                for azimuth in orders(degree):
                    k = rot_row(degree, azimuth, m)
                    term = rotf[k:k + 1, :] * dturned[slot(degree, azimuth), part, :]
                    total = term if total is None else total + term
                dxs[degree * degree + m, part, :] = total.astype(BF16)
        return carry

    lax.fori_loop(0, channels // BLOCK_C, turn_back, 0)
    advance(2, 3)
    advance(3, 3)
    advance(0, 4)
    advance(1, 4)

    d_target = dot(d_per_atom, weight(5), 1, 1)
    ext_grad = dot(src_hot, dxs[...].reshape(25 * channels, edges), 1, 1)
    grad_ref[...] = ext_grad[:atoms]
    grad_ref[:, :channels] = ext_grad[:atoms, :channels] + d_target
    for side in range(2):
        begin = atoms + side * slots
        ghost[side] = ext_grad[begin:begin + slots].astype(BF16)
    returns = [
        remote(ghost.at[0], back.at[0], side_send.at[2], side_recv.at[2], (row, left)),
        remote(ghost.at[1], back.at[1], side_send.at[3], side_recv.at[3], (row, right)),
    ]
    done = {0: 4, 1: 4, 2: 3, 3: 3, 4: 2, 5: 2, 6: 2, 7: 2}
    for i in (4, 5, 6, 7):
        done[i] += 1
        advance(i, done[i])
    att_ref[...] = dot(member_b, msg[...].reshape(25 * hidden, edges), 1, 1).astype(BF16)
    while any(done[i] < last_stage for i in done):
        for i in range(items):
            if done[i] < last_stage:
                done[i] += 1
                advance(i, done[i])

    for copy in returns:
        copy.wait_recv()
    total = grad_ref[...]
    for side, list_ref in ((0, right_ref), (1, left_ref)):
        ids = lax.broadcasted_iota(jnp.int32, (atoms, slots), 0)
        place = (ids == list_ref[...]).astype(F32).astype(BF16)
        total = total + dot(place, back[side], 1, 0)
    grad_ref[...] = total
    for i in range(items):
        for z in range(1, depth):
            flights["last", z, i].wait_recv()
    for copy in sides + returns + started:
        copy.wait_send()


def slab(n, depth, features, cotangent, rotation, src, tgt, send_left, send_right, weights):
    atoms = features.shape[0]
    edges = src.shape[1]
    slots = send_left.shape[1]
    heads = weights[6].shape[1]
    head_width = n * weights[6].shape[0]
    channels = n * weights[5].shape[0]
    hidden = weights[1].shape[1] // 4
    half = n // 2
    w_shapes = [tuple(w.shape) for w in weights]
    block = w_shapes[0][0]
    t_shapes = w_shapes[1:5] + [(block, 5 * hidden), (block, w_shapes[0][1] - 5 * hidden)]
    t_shapes += w_shapes[5:]
    sizes = {"weights": w_shapes, "terms": t_shapes}
    count, items = len(w_shapes), len(t_shapes)

    def layered(t):
        return (depth, t[0] if t[0] % depth else t[0] // depth, t[1])

    def lower(t):
        return (max(depth - 1, 1), *layered(t)[1:])

    shape = jax.ShapeDtypeStruct
    vmem = pl.BlockSpec(memory_space=pltpu.VMEM)
    out_shape = [shape((atoms, 25 * hidden), BF16), shape((atoms, 25 * channels), F32)]
    out_shape += [shape(layered(t), BF16) for t in t_shapes]
    rows = atoms + 2 * slots
    mixed = w_shapes[0][1]
    rots = rotation.shape[1]
    dma = pltpu.SemaphoreType.DMA
    scratch = [
        pltpu.VMEM((rows, 25 * channels), BF16),
        pltpu.VMEM((head_width, heads), F32),
        pltpu.VMEM((head_width, heads), F32),
        pltpu.VMEM((rots, edges), F32),
        pltpu.VMEM((25, channels, edges), F32),
        pltpu.VMEM((19, channels, edges), BF16),
        pltpu.VMEM((19, hidden, edges), F32),
        pltpu.VMEM((25, hidden, edges), BF16),
        pltpu.VMEM((25, hidden, edges), F32),
        pltpu.VMEM((head_width * heads, edges), F32),
        pltpu.VMEM((19, hidden, edges), BF16),
        pltpu.VMEM((mixed, edges), BF16),
        pltpu.VMEM((19, channels, edges), F32),
        pltpu.VMEM((25, channels, edges), BF16),
        pltpu.VMEM((2, heads, edges), F32),
        pltpu.VMEM((2, hidden, edges), F32),
    ]
    scratch += [pltpu.VMEM((2, slots, 25 * channels), BF16) for _ in range(4)]
    scratch += [pltpu.VMEM((half, 2, *w), BF16) for w in w_shapes]
    scratch += [pltpu.VMEM((n * w[0], w[1]) if w[0] % 16 else (8, 128), F32) for w in w_shapes]
    scratch += [pltpu.VMEM((half, 2, *t), BF16) for t in t_shapes]
    scratch += [pltpu.VMEM((half, *t), BF16) for t in t_shapes]
    scratch += [pltpu.VMEM((half - 1, *t), BF16) for _ in range(2) for t in t_shapes]
    scratch += [pltpu.VMEM(layered(t), F32) for t in t_shapes]
    scratch += [pltpu.VMEM(lower(t), BF16) for _ in range(2) for t in t_shapes]
    steps, deep = Halving(half).steps, Halving(depth).steps
    scratch += [dma((4,)) for _ in range(2)]
    scratch += [dma((half - 1, count)) for _ in range(2)]
    scratch += [dma((half, count)) for _ in range(2)]
    scratch += [dma((items,)) for _ in range(2)]
    scratch += [dma((steps, items)) for _ in range(2)]
    scratch += [dma((deep, items)) for _ in range(2)]
    scratch += [dma((depth, items)) for _ in range(2)]
    return pl.pallas_call(
        partial(slab_kernel, n, depth, sizes),
        out_shape=tuple(out_shape),
        in_specs=[vmem] * (7 + count),
        out_specs=[vmem] * (2 + items),
        scratch_shapes=scratch,
        compiler_params=pltpu.CompilerParams(
            collective_id=0, has_side_effects=True, vmem_limit_bytes=60 * 2**20),
        name="slab",
    )(features, cotangent, rotation, src, tgt, send_left, send_right, *weights)


def finish_kernel(items, hidden, *refs):
    att_ref, grad_ref = refs[:2]
    final = refs[2:2 + items]
    out_att, out_grad = refs[2 + items:4 + items]
    gz_ref, g1r_ref, g1i_ref, g2r_ref, g2i_ref, gt_ref, ga_ref = refs[4 + items:]
    out_att[...] = att_ref[...]
    out_grad[...] = grad_ref[...]

    def unfold(source, grad, begin):
        depth, size, wide = source.shape
        part = slice(begin, begin + wide)
        if size == grad.shape[0]:
            value = source[0].astype(F32)
            for k in range(1, depth):
                value = value + source[k].astype(F32)
            grad[:, part] = value
        else:
            for k in range(depth):
                grad[k * size:(k + 1) * size, part] = source[k].astype(F32)

    unfold(final[0], g1r_ref, 0)
    unfold(final[1], g1i_ref, 0)
    unfold(final[2], g2r_ref, 0)
    unfold(final[3], g2i_ref, 0)
    unfold(final[4], gz_ref, 0)
    unfold(final[5], gz_ref, 5 * hidden)
    unfold(final[6], gt_ref, 0)
    unfold(final[7], ga_ref, 0)


def finish(attended, grad, final, weights, hidden):
    items = len(final)
    vmem = pl.BlockSpec(memory_space=pltpu.VMEM)
    shapes = [jax.ShapeDtypeStruct(attended.shape, BF16), jax.ShapeDtypeStruct(grad.shape, F32)]
    shapes += [jax.ShapeDtypeStruct(w.shape, F32) for w in weights]
    return pl.pallas_call(
        partial(finish_kernel, items, hidden),
        out_shape=tuple(shapes),
        in_specs=[vmem] * (2 + items),
        out_specs=[vmem] * len(shapes),
        name="finish",
    )(attended, grad, *final)


def body(n, depth, features, cotangent, rotation, send_left, send_right, edge_src, edge_tgt,
         *weights):
    turned_rotation = jnp.swapaxes(rotation[0], 0, 1)
    attended, grad_features, *final = slab(
        n, depth, features[0], cotangent[0], turned_rotation, edge_src, edge_tgt,
        send_left, send_right, weights)
    attended, grad_features, *grads = finish(
        attended, grad_features, final, weights, weights[1].shape[1] // 4)
    return (attended[None], grad_features[None], *grads)


def solution(mesh):
    cell = P("dp", "graph", None)
    lists = P("dp", "graph")
    shard = P("graph", None)
    in_specs = (cell, cell, P("dp", None, "graph")) + (lists,) * 4 + (shard,) * 7
    out_specs = (cell, cell) + (shard,) * 7
    return jax.shard_map(
        partial(body, mesh.shape["graph"], mesh.shape["dp"]), mesh=mesh,
        in_specs=in_specs, out_specs=out_specs, check_vma=False)
```

time: 73.3 us -> 57.4 us (0.78)
  Pallas kernels: 70.8 us -> 56.6 us
  local copies, waits for them, and re-layouts: 1.54 us -> 0 us
    pallas_call x4 -> x2, Pallas kernels: 70.8 us -> 56.6 us  [the longest x1 54.5 us: slab(): pl.pallas_call(partial(slab_kernel, n, depth, sizes), out_shape=tuple(out...]
    unnamed x1 -> x0, local copies, waits for them, and re-layouts: 1.54 us -> none
where the time goes in v1:
time: 57.4 us; the launch traced here: 57.3 us
  Pallas kernels  56.6 us (99%)
  between operations  0.66 us (1%)
    pallas_call x1, Pallas kernels, slab(): pl.pallas_call(partial(slab_kernel, n, depth, sizes), out_shape=tuple(out...  54.5 us
    pallas_call x1, Pallas kernels, finish(): pl.pallas_call(partial(finish_kernel, items, hidden), out_shape=tuple(sha...  2.07 us

profile of v1, /device:TPU:0, one launch (start us, length us, event | category | flops | bytes accessed | tf_op | source)
XLA Modules:
  0.0 57.3 jit_solution(1007024922014188102)
XLA Ops:
  0.6 54.5 %slab.1 = (bf16[16,1600]{1,0:T(8,128)(2,1)}, f32[16,3200]{1,0:T(8,128)}, bf16[4,16,256]{2,1,0:T(8,128)(2,1)}, bf16[4,16,256]{2,1,0:T(8,128)(2,1)}, bf16[4,12,192...) custom-call(f32[16,3200]{1,0:T(8,128)} %bitcast.7, ...), custom_call_target="tpu_custom_call" | custom-call | tf_op jit(solution)/shard_map/slab/pallas_call | solution.py:627
  55.2 2.1 %finish.1 = (bf16[16,1600]{1,0:T(8,128)(2,1)}, f32[16,3200]{1,0:T(8,128)}, f32[80,832]{1,0:T(8,128)}, f32[64,256]{1,0:T(8,128)}, f32[64,256]{1,0:T(8,128)}, /*in...) custom-call(bf16[16,1600]{1,0:T(8,128)(2,1)} %get-tuple-element.28.refs_0_, ...), custom_call_target="tpu_custom_call" | custom-call | tf_op jit(solution)/shard_map/finish/pallas_call | solution.py:674

commit v2 on v1

--- a/solution.py
+++ b/solution.py
@@ -15,6 +15,13 @@
 BLOCK_H = 16
 MESH = pl.DeviceIdType.MESH
 EXACT = lax.Precision.HIGHEST
+ORDER = (
+    "g1r", "s0", "g1i", "s1", "gzv", "s3", "ds0", "s4", "x0", "ds1", "s5", "x1", "g2", "s2",
+    "x3", "gwt", "s6", "s7", "dt0", "dt1", "dt2", "x4", "tb0", "y0", "y1", "tb1", "eg", "y3",
+    "x5", "y4", "a0", "x2", "a1", "x6", "a3", "x7", "y5", "b0", "a4", "b1", "y2", "y6", "y7",
+    "ghost", "att", "a5", "b3", "c0", "b4", "a2", "c1", "a6", "a7", "b5", "d0", "c3", "b2",
+    "d1", "b6", "c4", "b7", "c5", "c2", "d3", "c6", "c7", "d4", "d5", "d2", "d6", "d7",
+)
 
 
 def slot(degree, azimuth):
@@ -87,7 +94,7 @@
     out_z = [next(take) for _ in range(items)]
     in_z = [next(take) for _ in range(items)]
     (side_send, side_recv, hop_send, hop_recv, core_send, core_recv, sib_send, sib_recv,
-     xy_send, xy_recv, z_send, z_recv, last_send, last_recv) = list(take)
+     xy_send, xy_recv, z_send, z_recv) = list(take)
 
     edges = src_ref.shape[1]
     rows = ext_ref.shape[0]
@@ -108,15 +115,26 @@
     plan = Halving(half)
     steps = plan.steps
     powers = [2 ** j + parity * (2 ** ((j + 1) % steps) - 2 ** j) for j in range(steps)]
-    deep = Halving(depth)
-    deep_powers = [2 ** j for j in range(deep.steps)]
+
+    upper = lax.div(row, depth // 2)
+    inward = row + 1 - 2 * upper
+    outward = row - 1 + 2 * upper
+    from_end = row + upper * (depth - 1 - 2 * row)
+    at_middle = lax.div(from_end + 1, depth // 2)
+    is_end = from_end == 0
+    is_middle = at_middle == 1
 
     barrier = pltpu.get_barrier_semaphore()
     partners = [(row, sibling), (row, right), (row, left)]
     partners += [(row, 2 * flip(chip, p) + parity) for p in powers]
-    partners += [(lax.rem(row + z, depth), me) for z in range(1, depth)]
     for partner in partners:
         pl.semaphore_signal(barrier, inc=1, device_id=partner, device_id_type=MESH)
+    for z in (-1, 1):
+        other = row + z
+
+        @pl.when((other >= 0) & (other < depth))
+        def _():
+            pl.semaphore_signal(barrier, inc=1, device_id=(other, me), device_id_type=MESH)
 
     def remote(src, dst, send, recv, target):
         copy = pltpu.make_async_remote_copy(
@@ -141,7 +159,7 @@
     member = (lax.broadcasted_iota(jnp.int32, (atoms, edges), 0) == tgt_ref[...]).astype(F32)
     member_b = member.astype(BF16)
 
-    pl.semaphore_wait(barrier, len(partners))
+    pl.semaphore_wait(barrier, len(partners) + 1 + lax.div(from_end + depth - 1, depth))
 
     sides = []
     for side, target in ((1, left), (0, right)):
@@ -333,18 +351,19 @@
 
     lax.fori_loop(0, hidden // BLOCK_H, mix, 0)
 
-    def put(i, value):
-        block, wide = sizes["terms"][i]
+    def put(i, value, begin=0):
+        block = sizes["terms"][i][0]
+        wide = value.shape[1]
         if block % 16:
             for u in range(half):
                 for c in range(2):
                     at = (2 * u + c) * block
-                    terms[i][u, c] = value[at:at + block, :].astype(BF16)
+                    terms[i][u, c, :, begin:begin + wide] = value[at:at + block, :].astype(BF16)
         else:
-            terms[i][...] = value.astype(BF16).reshape(half, 2, block, wide)
+            terms[i][:, :, :, begin:begin + wide] = value.astype(BF16).reshape(
+                half, 2, block, wide)
 
     flights = {}
-    even = [terms[i].shape[2] % depth == 0 for i in range(items)]
 
     def launch(key, src, dst, send, recv, target):
         copy = remote(src, dst, send, recv, target)
@@ -374,41 +393,55 @@
         launch(("xy", step, i), out_xy[i].at[begin:end], in_xy[i].at[begin:end],
                xy_send.at[step, i], xy_recv.at[step, i], target)
 
-    def layer_sum(i, step, chosen):
-        total = layers[i][flips(row, deep_powers, chosen)]
-        for s in range(step):
-            total = total + in_z[i][deep.spot(s, chosen)].astype(F32)
-        return total
-
-    def share(i):
-        for z in range(1, depth):
-            launch(("last", z, i), final[i].at[row], final[i].at[row], last_send.at[z, i],
-                   last_recv.at[z, i], (lax.rem(row + z, depth), me))
-
-    def to_layer(i, step):
-        if step == 0:
+    def inward_copy(i):
+        return pltpu.make_async_remote_copy(
+            src_ref=out_z[i], dst_ref=in_z[i].at[at_middle],
+            send_sem=z_send.at[0, i], recv_sem=z_recv.at[at_middle, i],
+            device_id=(inward, me), device_id_type=MESH)
+
+    def arrival(i, spot):
+        return pltpu.make_async_remote_copy(
+            src_ref=out_z[i], dst_ref=in_z[i].at[spot],
+            send_sem=z_send.at[0, i], recv_sem=z_recv.at[spot, i],
+            device_id=(inward, me), device_id_type=MESH)
+
+    def outward_copy(i):
+        return pltpu.make_async_remote_copy(
+            src_ref=final[i], dst_ref=final[i],
+            send_sem=z_send.at[1, i], recv_sem=z_recv.at[2, i],
+            device_id=(outward, me), device_id_type=MESH)
+
+    def on_line(i, stage):
+        if stage == 0:
             flights["xy", steps - 1, i].wait_recv()
             total = chip_sum(i, steps, ())
-            if not even[i]:
-                final[i][row] = total.astype(BF16)
-                share(i)
-                return
-            size = total.shape[0] // depth
-            for z in range(depth):
-                layers[i][z] = total[z * size:(z + 1) * size]
-        elif even[i]:
-            flights["z", step - 1, i].wait_recv()
-        if not even[i]:
-            return
-        if step == deep.steps:
-            final[i][row] = layer_sum(i, step, ()).astype(BF16)
-            share(i)
-            return
-        begin, end = deep.base[step], deep.base[step + 1]
-        for t, rest in enumerate(deep.rest[step]):
-            out_z[i][begin + t] = layer_sum(i, step, (step,) + rest).astype(BF16)
-        launch(("z", step, i), out_z[i].at[begin:end], in_z[i].at[begin:end],
-               z_send.at[step, i], z_recv.at[step, i], (flip(row, deep_powers[step]), me))
+            layers[i][...] = total
+            out_z[i][...] = total.astype(BF16)
+
+            @pl.when(is_end)
+            def _():
+                inward_copy(i).start()
+        elif stage == 1:
+            @pl.when(jnp.logical_not(is_end))
+            def _():
+                arrival(i, 0).wait_recv()
+                out_z[i][...] = (layers[i][...] + in_z[i][0].astype(F32)).astype(BF16)
+                inward_copy(i).start()
+        elif stage == 2:
+            @pl.when(is_middle)
+            def _():
+                arrival(i, 1).wait_recv()
+                final[i][...] = (out_z[i][...].astype(F32) + in_z[i][1].astype(F32)).astype(BF16)
+                if depth > 2:
+                    outward_copy(i).start()
+        else:
+            @pl.when(jnp.logical_not(is_middle))
+            def _():
+                outward_copy(i).wait_recv()
+                if depth > 4:
+                    @pl.when(jnp.logical_not(is_end))
+                    def _():
+                        outward_copy(i).start()
 
     def advance(i, stage):
         if stage == 0:
@@ -416,93 +449,81 @@
         elif stage <= steps:
             to_chip(i, stage - 1)
         else:
-            to_layer(i, stage - 1 - steps)
-
-    last_stage = steps + deep.steps + 1
-
-    def gradient_pair(first, number, re_item, im_item, pos, neg):
+            on_line(i, stage - 1 - steps)
+
+    def bands(first, number):
         middle = first + number
         last = middle + number
-        up = dhid[first:middle].reshape(number * hidden, edges)
-        down = dhid[middle:last].reshape(number * hidden, edges)
-        put(re_item, dot(pos, up, 1, 1) + dot(neg, down, 1, 1))
-        advance(re_item, 0)
-        put(im_item, dot(pos, down, 1, 1) - dot(neg, up, 1, 1))
-        advance(im_item, 0)
-
-    gradient_pair(5, 4, 0, 1, one_pos, one_neg)
-    gradient_pair(13, 3, 2, 3, two_pos, two_neg)
-    advance(0, 1)
-    advance(1, 1)
-    d_values = dhid[0:5].reshape(5 * hidden, edges)
-    dmixed[:5 * hidden, :] = d_values
-    put(4, dot(zero_in, d_values, 1, 1))
-    advance(4, 0)
-    advance(2, 1)
-    advance(3, 1)
-
-    d_weights = jnp.sum(
-        spreads[1].reshape(heads, hidden // heads, edges), axis=1
-    )
-    product = weights * d_weights
-    d_logits = product - weights * dot(
-        dot(product, member, 1, 1, EXACT), member, 1, 0, EXACT
-    )
-    small[0] = d_logits
-    for h in range(heads):
-        part = slice(h * width, (h + 1) * width)
-        normed = scores[part, :]
-        sig = jax.nn.sigmoid(normed)
-        gate = 0.2 + 0.8 * sig
-        d_logit = small[0, h:h + 1, :]
-        d_alphas[:, h:h + 1] = jnp.sum(normed * gate * d_logit, axis=1, keepdims=True)
-        d_norm = d_logit * alphas[:, h:h + 1] * (gate + 0.8 * normed * sig * (1.0 - sig))
-        first = jnp.mean(d_norm, axis=0, keepdims=True)
-        second = jnp.mean(d_norm * normed, axis=0, keepdims=True)
-        d_score = small[1, h:h + 1, :] * (d_norm - first - normed * second)
-        dmixed[5 * hidden + h * width:5 * hidden + (h + 1) * width, :] = d_score.astype(BF16)
-        scores[part, :] = d_score
-    put(5, dot(zero_in, dmixed[5 * hidden:, :], 1, 1))
-    advance(5, 0)
-    advance(4, 1)
-    d_per_atom = dot(member, scores[...], 1, 1, EXACT).astype(BF16)
-    put(6, dot(ext_ref[:atoms, :channels], d_per_atom, 0, 0))
-    advance(6, 0)
-    for u in range(half):
-        for c in range(2):
-            at = (2 * u + c) * alpha_rows
-            terms[7][u, c] = d_alphas[at:at + alpha_rows, :].astype(BF16)
-    advance(7, 0)
-    advance(0, 2)
-    advance(1, 2)
-    advance(5, 1)
-    advance(6, 1)
-    advance(7, 1)
-    advance(2, 2)
-    advance(3, 2)
-
-    dturned[0:5] = dot(weight(0), dmixed[...], 1, 0).reshape(5, channels, edges)
+        return (dhid[first:middle].reshape(number * hidden, edges),
+                dhid[middle:last].reshape(number * hidden, edges))
+
+    def one_re():
+        up, down = bands(5, 4)
+        put(0, dot(one_pos, up, 1, 1) + dot(one_neg, down, 1, 1))
+
+    def one_im():
+        up, down = bands(5, 4)
+        put(1, dot(one_pos, down, 1, 1) - dot(one_neg, up, 1, 1))
+
+    def two():
+        up, down = bands(13, 3)
+        put(2, dot(two_pos, up, 1, 1) + dot(two_neg, down, 1, 1))
+        put(2, dot(two_pos, down, 1, 1) - dot(two_neg, up, 1, 1), 3 * hidden)
+
+    def values():
+        d_values = dhid[0:5].reshape(5 * hidden, edges)
+        dmixed[:5 * hidden, :] = d_values
+        put(3, dot(zero_in, d_values, 1, 1))
+
+    def score_grads(which):
+        if which == 0:
+            d_weights = jnp.sum(
+                spreads[1].reshape(heads, hidden // heads, edges), axis=1
+            )
+            product = weights * d_weights
+            small[0] = product - weights * dot(
+                dot(product, member, 1, 1, EXACT), member, 1, 0, EXACT
+            )
+        group = heads // 2
+        for h in range(which * group, (which + 1) * group):
+            part = slice(h * width, (h + 1) * width)
+            normed = scores[part, :]
+            sig = jax.nn.sigmoid(normed)
+            gate = 0.2 + 0.8 * sig
+            d_logit = small[0, h:h + 1, :]
+            d_alphas[:, h:h + 1] = jnp.sum(normed * gate * d_logit, axis=1, keepdims=True)
+            d_norm = d_logit * alphas[:, h:h + 1] * (gate + 0.8 * normed * sig * (1.0 - sig))
+            first = jnp.mean(d_norm, axis=0, keepdims=True)
+            second = jnp.mean(d_norm * normed, axis=0, keepdims=True)
+            d_score = small[1, h:h + 1, :] * (d_norm - first - normed * second)
+            dmixed[5 * hidden + h * width:5 * hidden + (h + 1) * width, :] = d_score.astype(BF16)
+            scores[part, :] = d_score
+        begin = 5 * hidden + which * group * width
+        put(4 + which, dot(zero_in, dmixed[begin:begin + group * width, :], 1, 1))
+
+    held = {}
+
+    def target_alpha():
+        held["atom"] = dot(member, scores[...], 1, 1, EXACT).astype(BF16)
+        put(6, dot(ext_ref[:atoms, :channels], held["atom"], 0, 0))
+        for u in range(half):
+            for c in range(2):
+                at = (2 * u + c) * alpha_rows
+                terms[7][u, c] = d_alphas[at:at + alpha_rows, :].astype(BF16)
+
+    def turn_zero():
+        dturned[0:5] = dot(weight(0), dmixed[...], 1, 0).reshape(5, channels, edges)
 
     def turn_pair(first, number, re_item, im_item):
+        up, down = bands(first, number)
         middle = first + number
         last = middle + number
-        up = dhid[first:middle].reshape(number * hidden, edges)
-        down = dhid[middle:last].reshape(number * hidden, edges)
         dturned[first:middle] = (
             dot(weight(re_item), up, 1, 0) + dot(weight(im_item), down, 1, 0)
         ).reshape(number, channels, edges)
         dturned[middle:last] = (
             dot(weight(re_item), down, 1, 0) - dot(weight(im_item), up, 1, 0)
         ).reshape(number, channels, edges)
-
-    turn_pair(5, 4, 1, 2)
-    advance(0, 3)
-    advance(1, 3)
-    advance(4, 2)
-    advance(5, 2)
-    advance(6, 2)
-    advance(7, 2)
-    turn_pair(13, 3, 3, 4)
 
     def turn_back(i, carry):
         part = pl.ds(pl.multiple_of(i * BLOCK_C, BLOCK_C), BLOCK_C)
@@ -517,33 +538,47 @@
                 dxs[degree * degree + m, part, :] = total.astype(BF16)
         return carry
 
-    lax.fori_loop(0, channels // BLOCK_C, turn_back, 0)
-    advance(2, 3)
-    advance(3, 3)
-    advance(0, 4)
-    advance(1, 4)
-
-    d_target = dot(d_per_atom, weight(5), 1, 1)
-    ext_grad = dot(src_hot, dxs[...].reshape(25 * channels, edges), 1, 1)
-    grad_ref[...] = ext_grad[:atoms]
-    grad_ref[:, :channels] = ext_grad[:atoms, :channels] + d_target
-    for side in range(2):
-        begin = atoms + side * slots
-        ghost[side] = ext_grad[begin:begin + slots].astype(BF16)
-    returns = [
-        remote(ghost.at[0], back.at[0], side_send.at[2], side_recv.at[2], (row, left)),
-        remote(ghost.at[1], back.at[1], side_send.at[3], side_recv.at[3], (row, right)),
-    ]
-    done = {0: 4, 1: 4, 2: 3, 3: 3, 4: 2, 5: 2, 6: 2, 7: 2}
-    for i in (4, 5, 6, 7):
-        done[i] += 1
-        advance(i, done[i])
-    att_ref[...] = dot(member_b, msg[...].reshape(25 * hidden, edges), 1, 1).astype(BF16)
-    while any(done[i] < last_stage for i in done):
-        for i in range(items):
-            if done[i] < last_stage:
-                done[i] += 1
-                advance(i, done[i])
+    blocks = channels // BLOCK_C
+
+    def source_grads():
+        d_target = dot(held["atom"], weight(5), 1, 1)
+        ext_grad = dot(src_hot, dxs[...].reshape(25 * channels, edges), 1, 1)
+        grad_ref[...] = ext_grad[:atoms]
+        grad_ref[:, :channels] = ext_grad[:atoms, :channels] + d_target
+        for side in range(2):
+            begin = atoms + side * slots
+            ghost[side] = ext_grad[begin:begin + slots].astype(BF16)
+
+    returns = []
+
+    def return_ghosts():
+        for side, target in ((0, left), (1, right)):
+            returns.append(remote(ghost.at[side], back.at[side], side_send.at[2 + side],
+                                  side_recv.at[2 + side], (row, target)))
+
+    def attend():
+        att_ref[...] = dot(member_b, msg[...].reshape(25 * hidden, edges), 1, 1).astype(BF16)
+
+    work = {
+        "g1r": one_re, "g1i": one_im, "g2": two, "gzv": values,
+        "ds0": partial(score_grads, 0), "ds1": partial(score_grads, 1), "gwt": target_alpha,
+        "dt0": turn_zero, "dt1": partial(turn_pair, 5, 4, 1, 2),
+        "dt2": partial(turn_pair, 13, 3, 3, 4),
+        "tb0": lambda: lax.fori_loop(0, blocks // 2, turn_back, 0),
+        "tb1": lambda: lax.fori_loop(blocks // 2, blocks, turn_back, 0),
+        "eg": source_grads, "ghost": return_ghosts, "att": attend,
+    }
+    for step in ORDER:
+        if step in work:
+            work[step]()
+        else:
+            first, last = {
+                "s": (0, 1), "x": (1, 2), "y": (2, 1 + steps), "a": (1 + steps, 2 + steps),
+                "b": (2 + steps, 3 + steps), "c": (3 + steps, 4 + steps),
+                "d": (4 + steps, 5 + steps)}[step[0]]
+            for stage in range(first, last):
+                for i in step[1:]:
+                    advance(int(i), stage)
 
     for copy in returns:
         copy.wait_recv()
@@ -554,8 +589,11 @@
         total = total + dot(place, back[side], 1, 0)
     grad_ref[...] = total
     for i in range(items):
-        for z in range(1, depth):
-            flights["last", z, i].wait_recv()
+        inward_copy(i).wait_send()
+        if depth > 2:
+            @pl.when(jnp.logical_not(is_end))
+            def _():
+                outward_copy(i).wait_send()
     for copy in sides + returns + started:
         copy.wait_send()
 
@@ -571,21 +609,16 @@
     half = n // 2
     w_shapes = [tuple(w.shape) for w in weights]
     block = w_shapes[0][0]
-    t_shapes = w_shapes[1:5] + [(block, 5 * hidden), (block, w_shapes[0][1] - 5 * hidden)]
-    t_shapes += w_shapes[5:]
+    logits = (w_shapes[0][1] - 5 * hidden) // 2
+    t_shapes = w_shapes[1:3] + [(w_shapes[3][0], 6 * hidden), (block, 5 * hidden)]
+    t_shapes += [(block, logits)] * 2 + w_shapes[5:]
     sizes = {"weights": w_shapes, "terms": t_shapes}
     count, items = len(w_shapes), len(t_shapes)
-
-    def layered(t):
-        return (depth, t[0] if t[0] % depth else t[0] // depth, t[1])
-
-    def lower(t):
-        return (max(depth - 1, 1), *layered(t)[1:])
 
     shape = jax.ShapeDtypeStruct
     vmem = pl.BlockSpec(memory_space=pltpu.VMEM)
     out_shape = [shape((atoms, 25 * hidden), BF16), shape((atoms, 25 * channels), F32)]
-    out_shape += [shape(layered(t), BF16) for t in t_shapes]
+    out_shape += [shape(t, BF16) for t in t_shapes]
     rows = atoms + 2 * slots
     mixed = w_shapes[0][1]
     rots = rotation.shape[1]
@@ -614,16 +647,16 @@
     scratch += [pltpu.VMEM((half, 2, *t), BF16) for t in t_shapes]
     scratch += [pltpu.VMEM((half, *t), BF16) for t in t_shapes]
     scratch += [pltpu.VMEM((half - 1, *t), BF16) for _ in range(2) for t in t_shapes]
-    scratch += [pltpu.VMEM(layered(t), F32) for t in t_shapes]
-    scratch += [pltpu.VMEM(lower(t), BF16) for _ in range(2) for t in t_shapes]
-    steps, deep = Halving(half).steps, Halving(depth).steps
+    scratch += [pltpu.VMEM(t, F32) for t in t_shapes]
+    scratch += [pltpu.VMEM(t, BF16) for t in t_shapes]
+    scratch += [pltpu.VMEM((2, *t), BF16) for t in t_shapes]
+    steps = Halving(half).steps
     scratch += [dma((4,)) for _ in range(2)]
     scratch += [dma((half - 1, count)) for _ in range(2)]
     scratch += [dma((half, count)) for _ in range(2)]
     scratch += [dma((items,)) for _ in range(2)]
     scratch += [dma((steps, items)) for _ in range(2)]
-    scratch += [dma((deep, items)) for _ in range(2)]
-    scratch += [dma((depth, items)) for _ in range(2)]
+    scratch += [dma((2, items)), dma((3, items))]
     return pl.pallas_call(
         partial(slab_kernel, n, depth, sizes),
         out_shape=tuple(out_shape),
@@ -644,26 +677,18 @@
     out_att[...] = att_ref[...]
     out_grad[...] = grad_ref[...]
 
-    def unfold(source, grad, begin):
-        depth, size, wide = source.shape
-        part = slice(begin, begin + wide)
-        if size == grad.shape[0]:
-            value = source[0].astype(F32)
-            for k in range(1, depth):
-                value = value + source[k].astype(F32)
-            grad[:, part] = value
-        else:
-            for k in range(depth):
-                grad[k * size:(k + 1) * size, part] = source[k].astype(F32)
-
-    unfold(final[0], g1r_ref, 0)
-    unfold(final[1], g1i_ref, 0)
-    unfold(final[2], g2r_ref, 0)
-    unfold(final[3], g2i_ref, 0)
-    unfold(final[4], gz_ref, 0)
-    unfold(final[5], gz_ref, 5 * hidden)
-    unfold(final[6], gt_ref, 0)
-    unfold(final[7], ga_ref, 0)
+    wide = 3 * hidden
+    g1r_ref[...] = final[0][...].astype(F32)
+    g1i_ref[...] = final[1][...].astype(F32)
+    g2r_ref[...] = final[2][:, :wide].astype(F32)
+    g2i_ref[...] = final[2][:, wide:].astype(F32)
+    begin = 0
+    for source in final[3:6]:
+        end = begin + source.shape[1]
+        gz_ref[:, begin:end] = source[...].astype(F32)
+        begin = end
+    gt_ref[...] = final[6][...].astype(F32)
+    ga_ref[...] = final[7][...].astype(F32)
 
 
 def finish(attended, grad, final, weights, hidden):

time: 57.4 us -> 52.9 us (0.922)
  Pallas kernels: 56.6 us -> 52.1 us
    pallas_call x1, Pallas kernels: 54.5 us -> 50.2 us  [slab(): pl.pallas_call(partial(slab_kernel, n, depth, sizes), out_shape=tuple(out...]
where the time goes in v2:
time: 52.9 us; the launch traced here: 52.7 us
  Pallas kernels  52.1 us (98%)
  between operations  0.66 us (1%)
    pallas_call x1, Pallas kernels, slab(): pl.pallas_call(partial(slab_kernel, n, depth, sizes), out_shape=tuple(out...  50.2 us
    pallas_call x1, Pallas kernels, finish(): pl.pallas_call(partial(finish_kernel, items, hidden), out_shape=tuple(sha...  1.94 us

profile of v2, /device:TPU:0, one launch (start us, length us, event | category | flops | bytes accessed | tf_op | source)
XLA Modules:
  0.0 52.7 jit_solution(16498936848350519077)
XLA Ops:
  0.6 50.2 %slab.1 = (bf16[16,1600]{1,0:T(8,128)(2,1)}, f32[16,3200]{1,0:T(8,128)}, bf16[64,256]{1,0:T(8,128)(2,1)}, bf16[64,256]{1,0:T(8,128)(2,1)}, bf16[48,384]{1,0:T(8,...) custom-call(f32[16,3200]{1,0:T(8,128)} %bitcast.7, ...), custom_call_target="tpu_custom_call" | custom-call | tf_op jit(solution)/shard_map/slab/pallas_call | solution.py:660
  50.8 1.9 %finish.1 = (bf16[16,1600]{1,0:T(8,128)(2,1)}, f32[16,3200]{1,0:T(8,128)}, f32[80,832]{1,0:T(8,128)}, f32[64,256]{1,0:T(8,128)}, f32[64,256]{1,0:T(8,128)}, /*in...) custom-call(bf16[16,1600]{1,0:T(8,128)(2,1)} %get-tuple-element.28.refs_0_, ...), custom_call_target="tpu_custom_call" | custom-call | tf_op jit(solution)/shard_map/finish/pallas_call | solution.py:699

commit v3 on v2

--- a/solution.py
+++ b/solution.py
@@ -75,7 +75,7 @@
 
 def slab_kernel(n, depth, sizes, *refs):
     take = iter(refs)
-    feat_ref, cot_ref, rot_ref, src_ref, tgt_ref, left_ref, right_ref = [next(take) for _ in range(7)]
+    placed = [next(take) for _ in range(7)]
     count = len(sizes["weights"])
     items = len(sizes["terms"])
     shards = [next(take) for _ in range(count)]
@@ -94,7 +94,9 @@
     out_z = [next(take) for _ in range(items)]
     in_z = [next(take) for _ in range(items)]
     (side_send, side_recv, hop_send, hop_recv, core_send, core_recv, sib_send, sib_recv,
-     xy_send, xy_recv, z_send, z_recv) = list(take)
+     xy_send, xy_recv, z_send, z_recv, in_sem) = [next(take) for _ in range(13)]
+    local = list(take)
+    feat_ref, cot_ref, rot_ref, src_ref, tgt_ref, left_ref, right_ref = local
 
     edges = src_ref.shape[1]
     rows = ext_ref.shape[0]
@@ -145,6 +147,21 @@
 
     started = []
 
+    loads = {}
+
+    def load(key, src, dst, spot):
+        copy = pltpu.make_async_copy(src, dst, in_sem.at[spot])
+        copy.start()
+        loads[key] = copy
+
+    for k in (0, 5, 6):
+        load(k, placed[k], local[k], k)
+    for w in range(count):
+        load(("w", w), shards[w], full[w].at[chip, parity], 7 + w)
+    for k in (3, 4, 2, 1):
+        load(k, placed[k], local[k], k)
+    for k in (0, 5, 6):
+        loads[k].wait()
     own = feat_ref[...].astype(BF16)
     ext_ref[:atoms, :] = own
     for side, list_ref in ((0, left_ref), (1, right_ref)):
@@ -152,51 +169,56 @@
         pick = (ids == list_ref[...]).astype(F32).astype(BF16)
         outgoing[side] = dot(pick, own, 0, 0).astype(BF16)
     for w in range(count):
-        full[w][chip, parity] = shards[w][...]
+        loads["w", w].wait()
+
+    pl.semaphore_wait(barrier, len(partners) + 1 + lax.div(from_end + depth - 1, depth))
+
+    sides = []
+    for side, target in ((1, left), (0, right)):
+        sides.append(remote(outgoing.at[1 - side], near.at[side], side_send.at[side],
+                            side_recv.at[side], (row, target)))
+    arrivals = {}
+
+    def hop(j, w, part):
+        target = (row, 2 * flip(chip, powers[j]) + parity)
+        for t, chosen in enumerate(subsets(range(j))):
+            if (t > 0) != part:
+                continue
+            unit = flips(chip, powers, chosen)
+            copy = remote(full[w].at[unit, parity], full[w].at[unit, parity],
+                          hop_send.at[2 ** j + t - 1, w], hop_recv.at[2 ** j + t - 1, w], target)
+            arrivals[j, t, w] = copy
+            started.append(copy)
+
+    crossing = {}
+
+    def cross(spot, unit, w):
+        copy = remote(full[w].at[unit, parity], full[w].at[unit, parity],
+                      core_send.at[spot, w], core_recv.at[spot, w], (row, sibling))
+        crossing[spot, w] = copy
+        started.append(copy)
+
+    def land(j, w, part):
+        partner = flip(chip, powers[j])
+        for t, chosen in enumerate(subsets(range(j))):
+            if (t > 0) == part:
+                arrivals[j, t, w].wait_recv()
+                cross(2 ** j + t, flips(partner, powers, chosen), w)
+
+    weight_order = (0, 5, 6, 1, 2, 3, 4)
+    for j in range(steps):
+        for w in weight_order:
+            hop(j, w, False)
+    for w in weight_order:
+        cross(0, chip, w)
+
+    for k in (3, 4, 2, 1):
+        loads[k].wait()
     src_hot = (
         lax.broadcasted_iota(jnp.int32, (rows, edges), 0) == src_ref[...]
     ).astype(F32).astype(BF16)
     member = (lax.broadcasted_iota(jnp.int32, (atoms, edges), 0) == tgt_ref[...]).astype(F32)
     member_b = member.astype(BF16)
-
-    pl.semaphore_wait(barrier, len(partners) + 1 + lax.div(from_end + depth - 1, depth))
-
-    sides = []
-    for side, target in ((1, left), (0, right)):
-        sides.append(remote(outgoing.at[1 - side], near.at[side], side_send.at[side],
-                            side_recv.at[side], (row, target)))
-    arrivals = {}
-
-    def hop(j, w):
-        target = (row, 2 * flip(chip, powers[j]) + parity)
-        for t, chosen in enumerate(subsets(range(j))):
-            unit = flips(chip, powers, chosen)
-            source = shards[w] if j == 0 else full[w].at[unit, parity]
-            copy = remote(source, full[w].at[unit, parity], hop_send.at[2 ** j + t - 1, w],
-                          hop_recv.at[2 ** j + t - 1, w], target)
-            arrivals[j, t, w] = copy
-            started.append(copy)
-
-    crossing = {}
-
-    def cross(spot, unit, w, source=None):
-        copy = remote(full[w].at[unit, parity] if source is None else source,
-                      full[w].at[unit, parity], core_send.at[spot, w], core_recv.at[spot, w],
-                      (row, sibling))
-        crossing[spot, w] = copy
-        started.append(copy)
-
-    def land(j, w):
-        partner = flip(chip, powers[j])
-        for t, chosen in enumerate(subsets(range(j))):
-            arrivals[j, t, w].wait_recv()
-            cross(2 ** j + t, flips(partner, powers, chosen), w)
-
-    weight_order = (0, 5, 6, 1, 2, 3, 4)
-    for w in weight_order:
-        hop(0, w)
-    for w in weight_order:
-        cross(0, chip, w, shards[w])
 
     edge_eye = (
         lax.broadcasted_iota(jnp.int32, (rot_ref.shape[1], rot_ref.shape[1]), 0)
@@ -215,8 +237,9 @@
 
     for j in range(1, steps):
         for w in weight_order:
-            land(j - 1, w)
-            hop(j, w)
+            land(j - 1, w, False)
+            land(j - 1, w, True)
+            hop(j, w, True)
 
     def turn(i, carry):
         part = pl.ds(pl.multiple_of(i * BLOCK_C, BLOCK_C), BLOCK_C)
@@ -256,10 +279,10 @@
             return mats[w][:, begin:end].astype(BF16)
         return full[w][:, :, :, begin:end].reshape(n * block, end - begin)
 
-    for w in (0, 5, 6):
-        land(steps - 1, w)
-    for w in (1, 2):
-        land(steps - 1, w)
+    for w in weight_order:
+        land(steps - 1, w, False)
+    for w in (0, 5, 6, 1, 2):
+        land(steps - 1, w, True)
     for w in (0, 5, 6):
         settle(w)
     alpha_rows = sizes["weights"][6][0]
@@ -279,7 +302,7 @@
     hid[0:5] = dot(weight(0, 0, 5 * hidden), zero_in, 0, 0).reshape(5, hidden, edges)
 
     for w in (3, 4):
-        land(steps - 1, w)
+        land(steps - 1, w, True)
 
     for h in range(heads):
         part = slice(h * width, (h + 1) * width)
@@ -656,11 +679,13 @@
     scratch += [dma((half, count)) for _ in range(2)]
     scratch += [dma((items,)) for _ in range(2)]
     scratch += [dma((steps, items)) for _ in range(2)]
-    scratch += [dma((2, items)), dma((3, items))]
+    scratch += [dma((2, items)), dma((3, items)), dma((7 + count,))]
+    given = (features, cotangent, rotation, src, tgt, send_left, send_right)
+    scratch += [pltpu.VMEM(g.shape, g.dtype) for g in given]
     return pl.pallas_call(
         partial(slab_kernel, n, depth, sizes),
         out_shape=tuple(out_shape),
-        in_specs=[vmem] * (7 + count),
+        in_specs=[pl.BlockSpec(memory_space=pl.ANY)] * (7 + count),
         out_specs=[vmem] * (2 + items),
         scratch_shapes=scratch,
         compiler_params=pltpu.CompilerParams(

time: 52.9 us -> 51.8 us (0.979)
  Pallas kernels: 52.1 us -> 51 us
    pallas_call x1, Pallas kernels: 50.2 us -> 49 us  [slab(): pl.pallas_call(partial(slab_kernel, n, depth, sizes), out_shape=tuple(out...]
where the time goes in v3:
time: 51.8 us; the launch traced here: 51.6 us
  Pallas kernels  51 us (98%)
  between operations  0.66 us (1%)
    pallas_call x1, Pallas kernels, slab(): pl.pallas_call(partial(slab_kernel, n, depth, sizes), out_shape=tuple(out...  49 us
    pallas_call x1, Pallas kernels, finish(): pl.pallas_call(partial(finish_kernel, items, hidden), out_shape=tuple(sha...  1.94 us

profile of v3, /device:TPU:0, one launch (start us, length us, event | category | flops | bytes accessed | tf_op | source)
XLA Modules:
  0.0 51.6 jit_solution(17545722198089363294)
XLA Ops:
  0.6 49.0 %slab.1 = (bf16[16,1600]{1,0:T(8,128)(2,1)}, f32[16,3200]{1,0:T(8,128)}, bf16[64,256]{1,0:T(8,128)(2,1)}, bf16[64,256]{1,0:T(8,128)(2,1)}, bf16[48,384]{1,0:T(8,...) custom-call(f32[16,3200]{1,0:T(8,128)} %bitcast.7, ...), custom_call_target="tpu_custom_call" | custom-call | tf_op jit(solution)/shard_map/slab/pallas_call | solution.py:685
  49.7 1.9 %finish.1 = (bf16[16,1600]{1,0:T(8,128)(2,1)}, f32[16,3200]{1,0:T(8,128)}, f32[80,832]{1,0:T(8,128)}, f32[64,256]{1,0:T(8,128)}, f32[64,256]{1,0:T(8,128)}, /*in...) custom-call(bf16[16,1600]{1,0:T(8,128)(2,1)} %get-tuple-element.28.refs_0_, ...), custom_call_target="tpu_custom_call" | custom-call | tf_op jit(solution)/shard_map/finish/pallas_call | solution.py:724

commit v4 on v3

--- a/solution.py
+++ b/solution.py
@@ -17,11 +17,12 @@
 EXACT = lax.Precision.HIGHEST
 ORDER = (
     "g1r", "s0", "g1i", "s1", "gzv", "s3", "ds0", "s4", "x0", "ds1", "s5", "x1", "g2", "s2",
-    "x3", "gwt", "s6", "s7", "dt0", "dt1", "dt2", "x4", "tb0", "y0", "y1", "tb1", "eg", "y3",
+    "x3", "gwt", "s6", "s7", "dt0", "dt1", "dt2", "x4", "tb0", "y0", "y1", "tb1", "tb2", "tb3", "eg0", "eg1", "eg2", "eg3", "eg4", "y3",
     "x5", "y4", "a0", "x2", "a1", "x6", "a3", "x7", "y5", "b0", "a4", "b1", "y2", "y6", "y7",
     "ghost", "att", "a5", "b3", "c0", "b4", "a2", "c1", "a6", "a7", "b5", "d0", "c3", "b2",
     "d1", "b6", "c4", "b7", "c5", "c2", "d3", "c6", "c7", "d4", "d5", "d2", "d6", "d7",
 )
+TURN = (0, 1, 0, 0, 1, 1, 1, 1)
 
 
 def slot(degree, azimuth):
@@ -93,8 +94,9 @@
     layers = [next(take) for _ in range(items)]
     out_z = [next(take) for _ in range(items)]
     in_z = [next(take) for _ in range(items)]
+    whole = [next(take) for _ in range(items)]
     (side_send, side_recv, hop_send, hop_recv, core_send, core_recv, sib_send, sib_recv,
-     xy_send, xy_recv, z_send, z_recv, in_sem) = [next(take) for _ in range(13)]
+     xy_send, xy_recv, z_send, z_recv, end_send, end_recv, in_sem) = [next(take) for _ in range(15)]
     local = list(take)
     feat_ref, cot_ref, rot_ref, src_ref, tgt_ref, left_ref, right_ref = local
 
@@ -125,6 +127,8 @@
     at_middle = lax.div(from_end + 1, depth // 2)
     is_end = from_end == 0
     is_middle = at_middle == 1
+    odd = parity == 1
+    even = parity == 0
 
     barrier = pltpu.get_barrier_semaphore()
     partners = [(row, sibling), (row, right), (row, left)]
@@ -134,7 +138,7 @@
     for z in (-1, 1):
         other = row + z
 
-        @pl.when((other >= 0) & (other < depth))
+        @pl.when(odd & (other >= 0) & (other < depth))
         def _():
             pl.semaphore_signal(barrier, inc=1, device_id=(other, me), device_id_type=MESH)
 
@@ -171,7 +175,8 @@
     for w in range(count):
         loads["w", w].wait()
 
-    pl.semaphore_wait(barrier, len(partners) + 1 + lax.div(from_end + depth - 1, depth))
+    pl.semaphore_wait(
+        barrier, len(partners) + parity * (1 + lax.div(from_end + depth - 1, depth)))
 
     sides = []
     for side, target in ((1, left), (0, right)):
@@ -386,89 +391,96 @@
             terms[i][:, :, :, begin:begin + wide] = value.astype(BF16).reshape(
                 half, 2, block, wide)
 
-    flights = {}
-
-    def launch(key, src, dst, send, recv, target):
-        copy = remote(src, dst, send, recv, target)
-        flights[key] = copy
-        started.append(copy)
-
-    def to_sibling(i):
-        launch(("core", i), terms[i].at[:, 1 - parity], landed[i], sib_send.at[i], sib_recv.at[i],
-               (row, sibling))
+    def copy_to(src, dst, send, recv, target):
+        return pltpu.make_async_remote_copy(
+            src_ref=src, dst_ref=dst, send_sem=send, recv_sem=recv,
+            device_id=target, device_id_type=MESH)
+
+    def handed(i):
+        return copy_to(terms[i], landed[i], sib_send.at[i], sib_recv.at[i], (row, sibling))
+
+    def crossed(i, step):
+        begin, end = plan.base[step], plan.base[step + 1]
+        target = (row, 2 * flip(chip, order_of(i)[step]) + parity)
+        return copy_to(out_xy[i].at[begin:end], in_xy[i].at[begin:end],
+                       xy_send.at[step, i], xy_recv.at[step, i], target)
+
+    def inward_copy(i, spot):
+        return copy_to(out_z[i], in_z[i].at[spot], z_send.at[0, i], z_recv.at[spot, i],
+                       (inward, me))
+
+    def outward_copy(i):
+        return copy_to(whole[i], whole[i], z_send.at[1, i], z_recv.at[2, i], (outward, me))
+
+    def returned(i):
+        return copy_to(whole[i].at[0], final[i], end_send.at[i], end_recv.at[i], (row, sibling))
+
+    def order_of(i):
+        return [2 ** ((j + TURN[i]) % steps) for j in range(steps)]
 
     def chip_sum(i, step, chosen):
-        unit = flips(chip, powers, chosen)
-        total = terms[i][unit, parity].astype(F32) + landed[i][unit].astype(F32)
+        unit = flips(chip, order_of(i), chosen)
+        total = terms[i][unit].astype(F32) + landed[i][unit].astype(F32)
         for s in range(step):
             total = total + in_xy[i][plan.spot(s, chosen)].astype(F32)
         return total
 
     def to_chip(i, step):
-        if step == 0:
-            flights["core", i].wait_recv()
-        else:
-            flights["xy", step - 1, i].wait_recv()
-        begin, end = plan.base[step], plan.base[step + 1]
-        for t, rest in enumerate(plan.rest[step]):
-            out_xy[i][begin + t] = chip_sum(i, step, (step,) + rest).astype(BF16)
-        target = (row, 2 * flip(chip, powers[step]) + parity)
-        launch(("xy", step, i), out_xy[i].at[begin:end], in_xy[i].at[begin:end],
-               xy_send.at[step, i], xy_recv.at[step, i], target)
-
-    def inward_copy(i):
-        return pltpu.make_async_remote_copy(
-            src_ref=out_z[i], dst_ref=in_z[i].at[at_middle],
-            send_sem=z_send.at[0, i], recv_sem=z_recv.at[at_middle, i],
-            device_id=(inward, me), device_id_type=MESH)
-
-    def arrival(i, spot):
-        return pltpu.make_async_remote_copy(
-            src_ref=out_z[i], dst_ref=in_z[i].at[spot],
-            send_sem=z_send.at[0, i], recv_sem=z_recv.at[spot, i],
-            device_id=(inward, me), device_id_type=MESH)
-
-    def outward_copy(i):
-        return pltpu.make_async_remote_copy(
-            src_ref=final[i], dst_ref=final[i],
-            send_sem=z_send.at[1, i], recv_sem=z_recv.at[2, i],
-            device_id=(outward, me), device_id_type=MESH)
+        @pl.when(odd)
+        def _():
+            if step == 0:
+                handed(i).wait_recv()
+            else:
+                crossed(i, step - 1).wait_recv()
+            for t, rest in enumerate(plan.rest[step]):
+                out_xy[i][plan.base[step] + t] = chip_sum(i, step, (step,) + rest).astype(BF16)
+            crossed(i, step).start()
+
+    def finished(i):
+        returned(i).start()
+        final[i][...] = whole[i][1]
 
     def on_line(i, stage):
         if stage == 0:
-            flights["xy", steps - 1, i].wait_recv()
-            total = chip_sum(i, steps, ())
-            layers[i][...] = total
-            out_z[i][...] = total.astype(BF16)
-
-            @pl.when(is_end)
+            @pl.when(odd)
             def _():
-                inward_copy(i).start()
+                crossed(i, steps - 1).wait_recv()
+                total = chip_sum(i, steps, ())
+                layers[i][...] = total
+                out_z[i][...] = total.astype(BF16)
+
+                @pl.when(is_end)
+                def _():
+                    inward_copy(i, at_middle).start()
         elif stage == 1:
-            @pl.when(jnp.logical_not(is_end))
+            @pl.when(odd & jnp.logical_not(is_end))
             def _():
-                arrival(i, 0).wait_recv()
+                inward_copy(i, 0).wait_recv()
                 out_z[i][...] = (layers[i][...] + in_z[i][0].astype(F32)).astype(BF16)
-                inward_copy(i).start()
+                inward_copy(i, at_middle).start()
         elif stage == 2:
-            @pl.when(is_middle)
+            @pl.when(odd & is_middle)
             def _():
-                arrival(i, 1).wait_recv()
-                final[i][...] = (out_z[i][...].astype(F32) + in_z[i][1].astype(F32)).astype(BF16)
+                inward_copy(i, 1).wait_recv()
+                whole[i][...] = (out_z[i][...].astype(F32) + in_z[i][1].astype(F32)).astype(BF16)
                 if depth > 2:
                     outward_copy(i).start()
+                finished(i)
         else:
-            @pl.when(jnp.logical_not(is_middle))
+            @pl.when(odd & jnp.logical_not(is_middle))
             def _():
                 outward_copy(i).wait_recv()
                 if depth > 4:
                     @pl.when(jnp.logical_not(is_end))
                     def _():
                         outward_copy(i).start()
+                finished(i)
 
     def advance(i, stage):
         if stage == 0:
-            to_sibling(i)
+            @pl.when(even)
+            def _():
+                handed(i).start()
         elif stage <= steps:
             to_chip(i, stage - 1)
         else:
@@ -563,14 +575,16 @@
 
     blocks = channels // BLOCK_C
 
-    def source_grads():
-        d_target = dot(held["atom"], weight(5), 1, 1)
-        ext_grad = dot(src_hot, dxs[...].reshape(25 * channels, edges), 1, 1)
-        grad_ref[...] = ext_grad[:atoms]
-        grad_ref[:, :channels] = ext_grad[:atoms, :channels] + d_target
+    def source_grads(k):
+        part = slice(5 * k * channels, 5 * (k + 1) * channels)
+        ext_grad = dot(src_hot, dxs[5 * k:5 * k + 5].reshape(5 * channels, edges), 1, 1)
+        grad_ref[:, part] = ext_grad[:atoms]
+        if k == 0:
+            grad_ref[:, :channels] = ext_grad[:atoms, :channels] + dot(
+                held["atom"], weight(5), 1, 1)
         for side in range(2):
             begin = atoms + side * slots
-            ghost[side] = ext_grad[begin:begin + slots].astype(BF16)
+            ghost[side, :, part] = ext_grad[begin:begin + slots].astype(BF16)
 
     returns = []
 
@@ -587,10 +601,13 @@
         "ds0": partial(score_grads, 0), "ds1": partial(score_grads, 1), "gwt": target_alpha,
         "dt0": turn_zero, "dt1": partial(turn_pair, 5, 4, 1, 2),
         "dt2": partial(turn_pair, 13, 3, 3, 4),
-        "tb0": lambda: lax.fori_loop(0, blocks // 2, turn_back, 0),
-        "tb1": lambda: lax.fori_loop(blocks // 2, blocks, turn_back, 0),
-        "eg": source_grads, "ghost": return_ghosts, "att": attend,
+        "ghost": return_ghosts, "att": attend,
     }
+    for k in range(4):
+        work["tb%d" % k] = partial(
+            lax.fori_loop, k * blocks // 4, (k + 1) * blocks // 4, turn_back, 0)
+    for k in range(5):
+        work["eg%d" % k] = partial(source_grads, k)
     for step in ORDER:
         if step in work:
             work[step]()
@@ -611,12 +628,24 @@
         place = (ids == list_ref[...]).astype(F32).astype(BF16)
         total = total + dot(place, back[side], 1, 0)
     grad_ref[...] = total
-    for i in range(items):
-        inward_copy(i).wait_send()
-        if depth > 2:
-            @pl.when(jnp.logical_not(is_end))
-            def _():
-                outward_copy(i).wait_send()
+    @pl.when(even)
+    def _():
+        for i in range(items):
+            handed(i).wait_send()
+            returned(i).wait_recv()
+
+    @pl.when(odd)
+    def _():
+        for i in range(items):
+            for step in range(steps):
+                crossed(i, step).wait_send()
+            inward_copy(i, at_middle).wait_send()
+            if depth > 2:
+                @pl.when(jnp.logical_not(is_end))
+                def _():
+                    outward_copy(i).wait_send()
+            returned(i).wait_send()
+
     for copy in sides + returns + started:
         copy.wait_send()
 
@@ -668,10 +697,11 @@
     scratch += [pltpu.VMEM((half, 2, *w), BF16) for w in w_shapes]
     scratch += [pltpu.VMEM((n * w[0], w[1]) if w[0] % 16 else (8, 128), F32) for w in w_shapes]
     scratch += [pltpu.VMEM((half, 2, *t), BF16) for t in t_shapes]
-    scratch += [pltpu.VMEM((half, *t), BF16) for t in t_shapes]
-    scratch += [pltpu.VMEM((half - 1, *t), BF16) for _ in range(2) for t in t_shapes]
-    scratch += [pltpu.VMEM(t, F32) for t in t_shapes]
-    scratch += [pltpu.VMEM(t, BF16) for t in t_shapes]
+    scratch += [pltpu.VMEM((half, 2, *t), BF16) for t in t_shapes]
+    scratch += [pltpu.VMEM((half - 1, 2, *t), BF16) for _ in range(2) for t in t_shapes]
+    scratch += [pltpu.VMEM((2, *t), F32) for t in t_shapes]
+    scratch += [pltpu.VMEM((2, *t), BF16) for t in t_shapes]
+    scratch += [pltpu.VMEM((2, 2, *t), BF16) for t in t_shapes]
     scratch += [pltpu.VMEM((2, *t), BF16) for t in t_shapes]
     steps = Halving(half).steps
     scratch += [dma((4,)) for _ in range(2)]
@@ -679,7 +709,7 @@
     scratch += [dma((half, count)) for _ in range(2)]
     scratch += [dma((items,)) for _ in range(2)]
     scratch += [dma((steps, items)) for _ in range(2)]
-    scratch += [dma((2, items)), dma((3, items)), dma((7 + count,))]
+    scratch += [dma((2, items)), dma((3, items)), dma((items,)), dma((items,)), dma((7 + count,))]
     given = (features, cotangent, rotation, src, tgt, send_left, send_right)
     scratch += [pltpu.VMEM(g.shape, g.dtype) for g in given]
     return pl.pallas_call(

time: 51.8 us -> 52.3 us (level)
    pallas_call x1, Pallas kernels: 49 us -> 49.6 us  [slab(): pl.pallas_call(partial(slab_kernel, n, depth, sizes), out_shape=tuple(out...]
where the time goes in v4:
time: 52.3 us; the launch traced here: 52.2 us
  Pallas kernels  51.5 us (98%)
  between operations  0.66 us (1%)
    pallas_call x1, Pallas kernels, slab(): pl.pallas_call(partial(slab_kernel, n, depth, sizes), out_shape=tuple(out...  49.6 us
    pallas_call x1, Pallas kernels, finish(): pl.pallas_call(partial(finish_kernel, items, hidden), out_shape=tuple(sha...  1.94 us

profile of v4, /device:TPU:0, one launch (start us, length us, event | category | flops | bytes accessed | tf_op | source)
XLA Modules:
  0.0 52.2 jit_solution(18282084531322404077)
XLA Ops:
  0.6 49.6 %slab.1 = (bf16[16,1600]{1,0:T(8,128)(2,1)}, f32[16,3200]{1,0:T(8,128)}, bf16[64,256]{1,0:T(8,128)(2,1)}, bf16[64,256]{1,0:T(8,128)(2,1)}, bf16[48,384]{1,0:T(8,...) custom-call(f32[16,3200]{1,0:T(8,128)} %bitcast.7, ...), custom_call_target="tpu_custom_call" | custom-call | tf_op jit(solution)/shard_map/slab/pallas_call | solution.py:715
  50.2 1.9 %finish.1 = (bf16[16,1600]{1,0:T(8,128)(2,1)}, f32[16,3200]{1,0:T(8,128)}, f32[80,832]{1,0:T(8,128)}, f32[64,256]{1,0:T(8,128)}, f32[64,256]{1,0:T(8,128)}, /*in...) custom-call(bf16[16,1600]{1,0:T(8,128)(2,1)} %get-tuple-element.28.refs_0_, ...), custom_call_target="tpu_custom_call" | custom-call | tf_op jit(solution)/shard_map/finish/pallas_call | solution.py:754

commit v5 on v3

--- a/solution.py
+++ b/solution.py
@@ -16,12 +16,14 @@
 MESH = pl.DeviceIdType.MESH
 EXACT = lax.Precision.HIGHEST
 ORDER = (
-    "g1r", "s0", "g1i", "s1", "gzv", "s3", "ds0", "s4", "x0", "ds1", "s5", "x1", "g2", "s2",
-    "x3", "gwt", "s6", "s7", "dt0", "dt1", "dt2", "x4", "tb0", "y0", "y1", "tb1", "eg", "y3",
-    "x5", "y4", "a0", "x2", "a1", "x6", "a3", "x7", "y5", "b0", "a4", "b1", "y2", "y6", "y7",
-    "ghost", "att", "a5", "b3", "c0", "b4", "a2", "c1", "a6", "a7", "b5", "d0", "c3", "b2",
-    "d1", "b6", "c4", "b7", "c5", "c2", "d3", "c6", "c7", "d4", "d5", "d2", "d6", "d7",
+    "g1r", "s0", "g2", "s2", "ds0", "x0", "gzv", "s3", "x2", "g1i", "ds1", "s4", "s1", "x3",
+    "dt0", "gwt", "x4", "s7", "dt2", "y0", "s5", "dt1", "y2", "x1", "tb0", "s6", "y3", "x6",
+    "x5", "x7", "a0", "y4", "a2", "y1", "tb1", "tb2", "a3", "y6", "b0", "y5", "y7", "a4", "b2",
+    "tb3", "a6", "att", "b3", "a1", "a5", "b4", "c0", "eg0", "c2", "eg1", "a7", "b1", "b6",
+    "eg2", "eg3", "c3", "eg4", "b5", "ghost", "c4", "b7", "c1", "c6", "d3", "c5", "c7", "d0",
+    "d1",
 )
+CUBE = (2, 4, 5, 6, 7)
 
 
 def slot(degree, azimuth):
@@ -90,7 +92,6 @@
     landed = [next(take) for _ in range(items)]
     out_xy = [next(take) for _ in range(items)]
     in_xy = [next(take) for _ in range(items)]
-    layers = [next(take) for _ in range(items)]
     out_z = [next(take) for _ in range(items)]
     in_z = [next(take) for _ in range(items)]
     (side_send, side_recv, hop_send, hop_recv, core_send, core_recv, sib_send, sib_recv,
@@ -116,6 +117,8 @@
     right, left = lax.rem(me + 1, n), lax.rem(me + n - 1, n)
     plan = Halving(half)
     steps = plan.steps
+    deep = Halving(depth).steps
+    z_spots = max(deep, 2)
     powers = [2 ** j + parity * (2 ** ((j + 1) % steps) - 2 ** j) for j in range(steps)]
 
     upper = lax.div(row, depth // 2)
@@ -129,6 +132,7 @@
     barrier = pltpu.get_barrier_semaphore()
     partners = [(row, sibling), (row, right), (row, left)]
     partners += [(row, 2 * flip(chip, p) + parity) for p in powers]
+    partners += [(flip(row, 2 ** j), me) for j in range(deep)]
     for partner in partners:
         pl.semaphore_signal(barrier, inc=1, device_id=partner, device_id_type=MESH)
     for z in (-1, 1):
@@ -399,9 +403,9 @@
 
     def chip_sum(i, step, chosen):
         unit = flips(chip, powers, chosen)
-        total = terms[i][unit, parity].astype(F32) + landed[i][unit].astype(F32)
+        total = terms[i][unit, parity] + landed[i][unit]
         for s in range(step):
-            total = total + in_xy[i][plan.spot(s, chosen)].astype(F32)
+            total = total + in_xy[i][plan.spot(s, chosen)]
         return total
 
     def to_chip(i, step):
@@ -411,50 +415,51 @@
             flights["xy", step - 1, i].wait_recv()
         begin, end = plan.base[step], plan.base[step + 1]
         for t, rest in enumerate(plan.rest[step]):
-            out_xy[i][begin + t] = chip_sum(i, step, (step,) + rest).astype(BF16)
+            out_xy[i][begin + t] = chip_sum(i, step, (step,) + rest)
         target = (row, 2 * flip(chip, powers[step]) + parity)
         launch(("xy", step, i), out_xy[i].at[begin:end], in_xy[i].at[begin:end],
                xy_send.at[step, i], xy_recv.at[step, i], target)
 
-    def inward_copy(i):
+    def z_copy(i, out, spot, target):
         return pltpu.make_async_remote_copy(
-            src_ref=out_z[i], dst_ref=in_z[i].at[at_middle],
-            send_sem=z_send.at[0, i], recv_sem=z_recv.at[at_middle, i],
-            device_id=(inward, me), device_id_type=MESH)
-
-    def arrival(i, spot):
-        return pltpu.make_async_remote_copy(
-            src_ref=out_z[i], dst_ref=in_z[i].at[spot],
-            send_sem=z_send.at[0, i], recv_sem=z_recv.at[spot, i],
-            device_id=(inward, me), device_id_type=MESH)
+            src_ref=out_z[i].at[out], dst_ref=in_z[i].at[spot],
+            send_sem=z_send.at[out, i], recv_sem=z_recv.at[spot, i],
+            device_id=(target, me), device_id_type=MESH)
+
+    def inward_copy(i, spot):
+        return z_copy(i, 0, spot, inward)
+
+    def swap_copy(i, step):
+        return z_copy(i, step, step, flip(row, 2 ** step))
 
     def outward_copy(i):
         return pltpu.make_async_remote_copy(
             src_ref=final[i], dst_ref=final[i],
-            send_sem=z_send.at[1, i], recv_sem=z_recv.at[2, i],
+            send_sem=z_send.at[deep, i], recv_sem=z_recv.at[z_spots, i],
             device_id=(outward, me), device_id_type=MESH)
+
+    def layer_total(i):
+        flights["xy", steps - 1, i].wait_recv()
+        out_z[i][0] = chip_sum(i, steps, ())
 
     def on_line(i, stage):
         if stage == 0:
-            flights["xy", steps - 1, i].wait_recv()
-            total = chip_sum(i, steps, ())
-            layers[i][...] = total
-            out_z[i][...] = total.astype(BF16)
+            layer_total(i)
 
             @pl.when(is_end)
             def _():
-                inward_copy(i).start()
+                inward_copy(i, at_middle).start()
         elif stage == 1:
             @pl.when(jnp.logical_not(is_end))
             def _():
-                arrival(i, 0).wait_recv()
-                out_z[i][...] = (layers[i][...] + in_z[i][0].astype(F32)).astype(BF16)
-                inward_copy(i).start()
+                inward_copy(i, 0).wait_recv()
+                out_z[i][0] = out_z[i][0] + in_z[i][0]
+                inward_copy(i, at_middle).start()
         elif stage == 2:
             @pl.when(is_middle)
             def _():
-                arrival(i, 1).wait_recv()
-                final[i][...] = (out_z[i][...].astype(F32) + in_z[i][1].astype(F32)).astype(BF16)
+                inward_copy(i, 1).wait_recv()
+                final[i][...] = out_z[i][0] + in_z[i][1]
                 if depth > 2:
                     outward_copy(i).start()
         else:
@@ -466,13 +471,26 @@
                     def _():
                         outward_copy(i).start()
 
+    def on_cube(i, stage):
+        if stage == 0:
+            layer_total(i)
+            swap_copy(i, 0).start()
+        elif stage == 1:
+            for step in range(1, deep):
+                swap_copy(i, step - 1).wait_recv()
+                out_z[i][step] = out_z[i][step - 1] + in_z[i][step - 1]
+                swap_copy(i, step).start()
+        elif stage == 2:
+            swap_copy(i, deep - 1).wait_recv()
+            final[i][...] = out_z[i][deep - 1] + in_z[i][deep - 1]
+
     def advance(i, stage):
         if stage == 0:
             to_sibling(i)
         elif stage <= steps:
             to_chip(i, stage - 1)
         else:
-            on_line(i, stage - 1 - steps)
+            (on_cube if i in CUBE else on_line)(i, stage - 1 - steps)
 
     def bands(first, number):
         middle = first + number
@@ -563,14 +581,16 @@
 
     blocks = channels // BLOCK_C
 
-    def source_grads():
-        d_target = dot(held["atom"], weight(5), 1, 1)
-        ext_grad = dot(src_hot, dxs[...].reshape(25 * channels, edges), 1, 1)
-        grad_ref[...] = ext_grad[:atoms]
-        grad_ref[:, :channels] = ext_grad[:atoms, :channels] + d_target
+    def source_grads(k):
+        part = slice(5 * k * channels, 5 * (k + 1) * channels)
+        ext_grad = dot(src_hot, dxs[5 * k:5 * k + 5].reshape(5 * channels, edges), 1, 1)
+        grad_ref[:, part] = ext_grad[:atoms]
+        if k == 0:
+            grad_ref[:, :channels] = ext_grad[:atoms, :channels] + dot(
+                held["atom"], weight(5), 1, 1)
         for side in range(2):
             begin = atoms + side * slots
-            ghost[side] = ext_grad[begin:begin + slots].astype(BF16)
+            ghost[side, :, part] = ext_grad[begin:begin + slots].astype(BF16)
 
     returns = []
 
@@ -587,10 +607,13 @@
         "ds0": partial(score_grads, 0), "ds1": partial(score_grads, 1), "gwt": target_alpha,
         "dt0": turn_zero, "dt1": partial(turn_pair, 5, 4, 1, 2),
         "dt2": partial(turn_pair, 13, 3, 3, 4),
-        "tb0": lambda: lax.fori_loop(0, blocks // 2, turn_back, 0),
-        "tb1": lambda: lax.fori_loop(blocks // 2, blocks, turn_back, 0),
-        "eg": source_grads, "ghost": return_ghosts, "att": attend,
+        "ghost": return_ghosts, "att": attend,
     }
+    for k in range(4):
+        work["tb%d" % k] = partial(
+            lax.fori_loop, k * blocks // 4, (k + 1) * blocks // 4, turn_back, 0)
+    for k in range(5):
+        work["eg%d" % k] = partial(source_grads, k)
     for step in ORDER:
         if step in work:
             work[step]()
@@ -612,7 +635,11 @@
         total = total + dot(place, back[side], 1, 0)
     grad_ref[...] = total
     for i in range(items):
-        inward_copy(i).wait_send()
+        if i in CUBE:
+            for step in range(deep):
+                swap_copy(i, step).wait_send()
+            continue
+        inward_copy(i, at_middle).wait_send()
         if depth > 2:
             @pl.when(jnp.logical_not(is_end))
             def _():
@@ -670,16 +697,15 @@
     scratch += [pltpu.VMEM((half, 2, *t), BF16) for t in t_shapes]
     scratch += [pltpu.VMEM((half, *t), BF16) for t in t_shapes]
     scratch += [pltpu.VMEM((half - 1, *t), BF16) for _ in range(2) for t in t_shapes]
-    scratch += [pltpu.VMEM(t, F32) for t in t_shapes]
-    scratch += [pltpu.VMEM(t, BF16) for t in t_shapes]
-    scratch += [pltpu.VMEM((2, *t), BF16) for t in t_shapes]
-    steps = Halving(half).steps
+    steps, deep = Halving(half).steps, Halving(depth).steps
+    scratch += [pltpu.VMEM((deep, *t), BF16) for t in t_shapes]
+    scratch += [pltpu.VMEM((max(deep, 2), *t), BF16) for t in t_shapes]
     scratch += [dma((4,)) for _ in range(2)]
     scratch += [dma((half - 1, count)) for _ in range(2)]
     scratch += [dma((half, count)) for _ in range(2)]
     scratch += [dma((items,)) for _ in range(2)]
     scratch += [dma((steps, items)) for _ in range(2)]
-    scratch += [dma((2, items)), dma((3, items)), dma((7 + count,))]
+    scratch += [dma((deep + 1, items)), dma((max(deep, 2) + 1, items)), dma((7 + count,))]
     given = (features, cotangent, rotation, src, tgt, send_left, send_right)
     scratch += [pltpu.VMEM(g.shape, g.dtype) for g in given]
     return pl.pallas_call(

time: 51.8 us -> 51 us (0.985)
  Pallas kernels: 51 us -> 50.2 us
    pallas_call x1, Pallas kernels: 49 us -> 48.3 us  [slab(): pl.pallas_call(partial(slab_kernel, n, depth, sizes), out_shape=tuple(out...]
where the time goes in v5:
time: 51 us; the launch traced here: 50.9 us
  Pallas kernels  50.2 us (98%)
  between operations  0.66 us (1%)
    pallas_call x1, Pallas kernels, slab(): pl.pallas_call(partial(slab_kernel, n, depth, sizes), out_shape=tuple(out...  48.3 us
    pallas_call x1, Pallas kernels, finish(): pl.pallas_call(partial(finish_kernel, items, hidden), out_shape=tuple(sha...  1.94 us

profile of v5, /device:TPU:0, one launch (start us, length us, event | category | flops | bytes accessed | tf_op | source)
XLA Modules:
  0.0 50.9 jit_solution(10692393849754988150)
XLA Ops:
  0.6 48.3 %slab.1 = (bf16[16,1600]{1,0:T(8,128)(2,1)}, f32[16,3200]{1,0:T(8,128)}, bf16[64,256]{1,0:T(8,128)(2,1)}, bf16[64,256]{1,0:T(8,128)(2,1)}, bf16[48,384]{1,0:T(8,...) custom-call(f32[16,3200]{1,0:T(8,128)} %bitcast.7, ...), custom_call_target="tpu_custom_call" | custom-call | tf_op jit(solution)/shard_map/slab/pallas_call | solution.py:711
  48.9 1.9 %finish.1 = (bf16[16,1600]{1,0:T(8,128)(2,1)}, f32[16,3200]{1,0:T(8,128)}, f32[80,832]{1,0:T(8,128)}, f32[64,256]{1,0:T(8,128)}, f32[64,256]{1,0:T(8,128)}, /*in...) custom-call(bf16[16,1600]{1,0:T(8,128)(2,1)} %get-tuple-element.28.refs_0_, ...), custom_call_target="tpu_custom_call" | custom-call | tf_op jit(solution)/shard_map/finish/pallas_call | solution.py:750

commit v6 on v5

--- a/solution.py
+++ b/solution.py
@@ -20,8 +20,8 @@
     "dt0", "gwt", "x4", "s7", "dt2", "y0", "s5", "dt1", "y2", "x1", "tb0", "s6", "y3", "x6",
     "x5", "x7", "a0", "y4", "a2", "y1", "tb1", "tb2", "a3", "y6", "b0", "y5", "y7", "a4", "b2",
     "tb3", "a6", "att", "b3", "a1", "a5", "b4", "c0", "eg0", "c2", "eg1", "a7", "b1", "b6",
-    "eg2", "eg3", "c3", "eg4", "b5", "ghost", "c4", "b7", "c1", "c6", "d3", "c5", "c7", "d0",
-    "d1",
+    "eg2", "eg3", "c3", "eg4", "b5", "ghost", "c4", "b7", "c1", "c6", "d3", "add", "c5", "c7",
+    "d0", "d1",
 )
 CUBE = (2, 4, 5, 6, 7)
 
@@ -81,8 +81,7 @@
     count = len(sizes["weights"])
     items = len(sizes["terms"])
     shards = [next(take) for _ in range(count)]
-    att_ref, grad_ref = next(take), next(take)
-    final = [next(take) for _ in range(items)]
+    results = [next(take) for _ in range(2 + items)]
     (ext_ref, alphas, d_alphas, rotf, xs, turned, hid, msg, dmsg, scores, dhid, dmixed, dturned,
      dxs, small, spreads) = [next(take) for _ in range(16)]
     outgoing, near, ghost, back = [next(take) for _ in range(4)]
@@ -95,8 +94,11 @@
     out_z = [next(take) for _ in range(items)]
     in_z = [next(take) for _ in range(items)]
     (side_send, side_recv, hop_send, hop_recv, core_send, core_recv, sib_send, sib_recv,
-     xy_send, xy_recv, z_send, z_recv, in_sem) = [next(take) for _ in range(13)]
-    local = list(take)
+     xy_send, xy_recv, z_send, z_recv, in_sem, out_sem) = [next(take) for _ in range(14)]
+    local = [next(take) for _ in range(7)]
+    leaving = list(take)
+    att_ref, grad_ref = leaving[:2]
+    final = leaving[2:]
     feat_ref, cot_ref, rot_ref, src_ref, tgt_ref, left_ref, right_ref = local
 
     edges = src_ref.shape[1]
@@ -438,6 +440,9 @@
             send_sem=z_send.at[deep, i], recv_sem=z_recv.at[z_spots, i],
             device_id=(outward, me), device_id_type=MESH)
 
+    def leave(k):
+        return pltpu.make_async_copy(leaving[k], results[k], out_sem.at[k])
+
     def layer_total(i):
         flights["xy", steps - 1, i].wait_recv()
         out_z[i][0] = chip_sum(i, steps, ())
@@ -460,6 +465,7 @@
             def _():
                 inward_copy(i, 1).wait_recv()
                 final[i][...] = out_z[i][0] + in_z[i][1]
+                leave(2 + i).start()
                 if depth > 2:
                     outward_copy(i).start()
         else:
@@ -470,6 +476,7 @@
                     @pl.when(jnp.logical_not(is_end))
                     def _():
                         outward_copy(i).start()
+                leave(2 + i).start()
 
     def on_cube(i, stage):
         if stage == 0:
@@ -483,6 +490,7 @@
         elif stage == 2:
             swap_copy(i, deep - 1).wait_recv()
             final[i][...] = out_z[i][deep - 1] + in_z[i][deep - 1]
+            leave(2 + i).start()
 
     def advance(i, stage):
         if stage == 0:
@@ -601,13 +609,25 @@
 
     def attend():
         att_ref[...] = dot(member_b, msg[...].reshape(25 * hidden, edges), 1, 1).astype(BF16)
+        leave(0).start()
+
+    def add_ghosts():
+        for copy in returns:
+            copy.wait_recv()
+        total = grad_ref[...]
+        for side, list_ref in ((0, right_ref), (1, left_ref)):
+            ids = lax.broadcasted_iota(jnp.int32, (atoms, slots), 0)
+            place = (ids == list_ref[...]).astype(F32).astype(BF16)
+            total = total + dot(place, back[side], 1, 0)
+        grad_ref[...] = total
+        leave(1).start()
 
     work = {
         "g1r": one_re, "g1i": one_im, "g2": two, "gzv": values,
         "ds0": partial(score_grads, 0), "ds1": partial(score_grads, 1), "gwt": target_alpha,
         "dt0": turn_zero, "dt1": partial(turn_pair, 5, 4, 1, 2),
         "dt2": partial(turn_pair, 13, 3, 3, 4),
-        "ghost": return_ghosts, "att": attend,
+        "ghost": return_ghosts, "add": add_ghosts, "att": attend,
     }
     for k in range(4):
         work["tb%d" % k] = partial(
@@ -626,14 +646,6 @@
                 for i in step[1:]:
                     advance(int(i), stage)
 
-    for copy in returns:
-        copy.wait_recv()
-    total = grad_ref[...]
-    for side, list_ref in ((0, right_ref), (1, left_ref)):
-        ids = lax.broadcasted_iota(jnp.int32, (atoms, slots), 0)
-        place = (ids == list_ref[...]).astype(F32).astype(BF16)
-        total = total + dot(place, back[side], 1, 0)
-    grad_ref[...] = total
     for i in range(items):
         if i in CUBE:
             for step in range(deep):
@@ -646,6 +658,8 @@
                 outward_copy(i).wait_send()
     for copy in sides + returns + started:
         copy.wait_send()
+    for k in range(2 + items):
+        leave(k).wait()
 
 
 def slab(n, depth, features, cotangent, rotation, src, tgt, send_left, send_right, weights):
@@ -707,12 +721,13 @@
     scratch += [dma((steps, items)) for _ in range(2)]
     scratch += [dma((deep + 1, items)), dma((max(deep, 2) + 1, items)), dma((7 + count,))]
     given = (features, cotangent, rotation, src, tgt, send_left, send_right)
-    scratch += [pltpu.VMEM(g.shape, g.dtype) for g in given]
+    scratch += [dma((2 + items,))]
+    scratch += [pltpu.VMEM(g.shape, g.dtype) for g in (*given, *out_shape)]
     return pl.pallas_call(
         partial(slab_kernel, n, depth, sizes),
         out_shape=tuple(out_shape),
         in_specs=[pl.BlockSpec(memory_space=pl.ANY)] * (7 + count),
-        out_specs=[vmem] * (2 + items),
+        out_specs=[pl.BlockSpec(memory_space=pl.ANY)] * (2 + items),
         scratch_shapes=scratch,
         compiler_params=pltpu.CompilerParams(
             collective_id=0, has_side_effects=True, vmem_limit_bytes=60 * 2**20),

time: 51 us -> 50.6 us (level)
  no operation moved by 1% of the time
where the time goes in v6:
time: 50.6 us; the launch traced here: 50.5 us
  Pallas kernels  49.8 us (98%)
  between operations  0.66 us (1%)
    pallas_call x1, Pallas kernels, slab(): pl.pallas_call(partial(slab_kernel, n, depth, sizes), out_shape=tuple(out...  47.9 us
    pallas_call x1, Pallas kernels, finish(): pl.pallas_call(partial(finish_kernel, items, hidden), out_shape=tuple(sha...  1.94 us

profile of v6, /device:TPU:0, one launch (start us, length us, event | category | flops | bytes accessed | tf_op | source)
XLA Modules:
  0.0 50.5 jit_solution(7727649131769412112)
XLA Ops:
  0.6 47.9 %slab.1 = (bf16[16,1600]{1,0:T(8,128)(2,1)}, f32[16,3200]{1,0:T(8,128)}, bf16[64,256]{1,0:T(8,128)(2,1)}, bf16[64,256]{1,0:T(8,128)(2,1)}, bf16[48,384]{1,0:T(8,...) custom-call(f32[16,3200]{1,0:T(8,128)} %bitcast.7, ...), custom_call_target="tpu_custom_call" | custom-call | tf_op jit(solution)/shard_map/slab/pallas_call | solution.py:726
  48.5 1.9 %finish.1 = (bf16[16,1600]{1,0:T(8,128)(2,1)}, f32[16,3200]{1,0:T(8,128)}, f32[80,832]{1,0:T(8,128)}, f32[64,256]{1,0:T(8,128)}, f32[64,256]{1,0:T(8,128)}, /*in...) custom-call(bf16[16,1600]{1,0:T(8,128)(2,1)} %get-tuple-element.28.refs_0_, ...), custom_call_target="tpu_custom_call" | custom-call | tf_op jit(solution)/shard_map/finish/pallas_call | solution.py:765

commit v7 on v6

--- a/solution.py
+++ b/solution.py
@@ -11,7 +11,7 @@
 BF16 = jnp.bfloat16
 OFFSETS = {1: 0, 2: 9, 3: 34, 4: 69}
 DEGREES = (1, 2, 3, 4)
-BLOCK_C = 32
+BLOCK_C = 16
 BLOCK_H = 16
 MESH = pl.DeviceIdType.MESH
 EXACT = lax.Precision.HIGHEST
@@ -73,6 +73,17 @@
 
     def spot(self, step, chosen):
         return self.base[step] + self.rest[step].index(chosen)
+
+
+def pieces_of(shapes):
+    found = []
+    for w, (block, _) in enumerate(shapes):
+        cut = block // 32 * 16
+        if w == 0 and block % 16 == 0 and cut:
+            found += [(w, 0, cut), (w, cut, block)]
+        else:
+            found.append((w, 0, block))
+    return found
 
 
 def slab_kernel(n, depth, sizes, *refs):
@@ -185,13 +196,21 @@
                             side_recv.at[side], (row, target)))
     arrivals = {}
 
+    pieces = pieces_of(sizes["weights"])
+
+    def block_of(w, unit):
+        own, begin, end = pieces[w]
+        if end - begin == sizes["weights"][own][0]:
+            return full[own].at[unit, parity]
+        return full[own].at[unit, parity, begin:end]
+
     def hop(j, w, part):
         target = (row, 2 * flip(chip, powers[j]) + parity)
         for t, chosen in enumerate(subsets(range(j))):
             if (t > 0) != part:
                 continue
             unit = flips(chip, powers, chosen)
-            copy = remote(full[w].at[unit, parity], full[w].at[unit, parity],
+            copy = remote(block_of(w, unit), block_of(w, unit),
                           hop_send.at[2 ** j + t - 1, w], hop_recv.at[2 ** j + t - 1, w], target)
             arrivals[j, t, w] = copy
             started.append(copy)
@@ -199,7 +218,7 @@
     crossing = {}
 
     def cross(spot, unit, w):
-        copy = remote(full[w].at[unit, parity], full[w].at[unit, parity],
+        copy = remote(block_of(w, unit), block_of(w, unit),
                       core_send.at[spot, w], core_recv.at[spot, w], (row, sibling))
         crossing[spot, w] = copy
         started.append(copy)
@@ -211,7 +230,8 @@
                 arrivals[j, t, w].wait_recv()
                 cross(2 ** j + t, flips(partner, powers, chosen), w)
 
-    weight_order = (0, 5, 6, 1, 2, 3, 4)
+    weight_order = [p for w in (0, 5, 6, 1, 2, 3, 4)
+                    for p in range(len(pieces)) if pieces[p][0] == w]
     for j in range(steps):
         for w in weight_order:
             hop(j, w, False)
@@ -270,7 +290,9 @@
 
     def settle(w):
         for spot in range(half):
-            crossing[spot, w].wait_recv()
+            for p in range(len(pieces)):
+                if pieces[p][0] == w:
+                    crossing[spot, p].wait_recv()
         block = sizes["weights"][w][0]
         if block % 16:
             for u in range(half):
@@ -287,8 +309,9 @@
 
     for w in weight_order:
         land(steps - 1, w, False)
-    for w in (0, 5, 6, 1, 2):
-        land(steps - 1, w, True)
+    for w in weight_order:
+        if pieces[w][0] not in (3, 4):
+            land(steps - 1, w, True)
     for w in (0, 5, 6):
         settle(w)
     alpha_rows = sizes["weights"][6][0]
@@ -307,8 +330,9 @@
     )
     hid[0:5] = dot(weight(0, 0, 5 * hidden), zero_in, 0, 0).reshape(5, hidden, edges)
 
-    for w in (3, 4):
-        land(steps - 1, w, True)
+    for w in weight_order:
+        if pieces[w][0] in (3, 4):
+            land(steps - 1, w, True)
 
     for h in range(heads):
         part = slice(h * width, (h + 1) * width)
@@ -715,8 +739,9 @@
     scratch += [pltpu.VMEM((deep, *t), BF16) for t in t_shapes]
     scratch += [pltpu.VMEM((max(deep, 2), *t), BF16) for t in t_shapes]
     scratch += [dma((4,)) for _ in range(2)]
-    scratch += [dma((half - 1, count)) for _ in range(2)]
-    scratch += [dma((half, count)) for _ in range(2)]
+    parts = len(pieces_of(w_shapes))
+    scratch += [dma((half - 1, parts)) for _ in range(2)]
+    scratch += [dma((half, parts)) for _ in range(2)]
     scratch += [dma((items,)) for _ in range(2)]
     scratch += [dma((steps, items)) for _ in range(2)]
     scratch += [dma((deep + 1, items)), dma((max(deep, 2) + 1, items)), dma((7 + count,))]

time: 50.6 us -> 50.7 us (level)
  no operation moved by 1% of the time
where the time goes in v7:
time: 50.7 us; the launch traced here: 50.6 us
  Pallas kernels  49.9 us (98%)
  between operations  0.66 us (1%)
    pallas_call x1, Pallas kernels, slab(): pl.pallas_call(partial(slab_kernel, n, depth, sizes), out_shape=tuple(out...  48 us
    pallas_call x1, Pallas kernels, finish(): pl.pallas_call(partial(finish_kernel, items, hidden), out_shape=tuple(sha...  1.94 us

profile of v7, /device:TPU:0, one launch (start us, length us, event | category | flops | bytes accessed | tf_op | source)
XLA Modules:
  0.0 50.6 jit_solution(14902222742016601874)
XLA Ops:
  0.6 48.0 %slab.1 = (bf16[16,1600]{1,0:T(8,128)(2,1)}, f32[16,3200]{1,0:T(8,128)}, bf16[64,256]{1,0:T(8,128)(2,1)}, bf16[64,256]{1,0:T(8,128)(2,1)}, bf16[48,384]{1,0:T(8,...) custom-call(f32[16,3200]{1,0:T(8,128)} %bitcast.7, ...), custom_call_target="tpu_custom_call" | custom-call | tf_op jit(solution)/shard_map/slab/pallas_call | solution.py:751
  48.6 1.9 %finish.1 = (bf16[16,1600]{1,0:T(8,128)(2,1)}, f32[16,3200]{1,0:T(8,128)}, f32[80,832]{1,0:T(8,128)}, f32[64,256]{1,0:T(8,128)}, f32[64,256]{1,0:T(8,128)}, /*in...) custom-call(bf16[16,1600]{1,0:T(8,128)(2,1)} %get-tuple-element.28.refs_0_, ...), custom_call_target="tpu_custom_call" | custom-call | tf_op jit(solution)/shard_map/finish/pallas_call | solution.py:790
